TPU v7x, 32 devices: a whole 2x2x4 slice. The times are simulated.
32 devices in a mesh: fsdp: 8 (over z, x), tensor: 2 (over y), dp: 2 (over core).
Axes of the slice: x: 2, y: 2, z: 4, core: 2. Of those that a mesh axis runs over, the one named last changes fastest.
Arguments:
- states: bfloat16 [4096, 4096], P('fsdp', ('tensor', 'dp')), may hold values from -6 to 6
- fresh_rows: bfloat16 [4096, 4096], P('fsdp', ('tensor', 'dp')), may hold values from -6 to 6
- norm_gain: bfloat16 [4096], P(('tensor', 'dp')), may hold values from 0.25 to 1.75
- gate_weight: bfloat16 [4096, 8192], P('fsdp', ('tensor', 'dp')), may hold values from -0.09375 to 0.09375
- up_weight: bfloat16 [4096, 8192], P('fsdp', ('tensor', 'dp')), may hold values from -0.09375 to 0.09375
- down_weight: bfloat16 [8192, 4096], P(('tensor', 'dp'), 'fsdp'), may hold values from -0.09375 to 0.09375
- halted: int32 [64, 64], P('fsdp'), may hold values from 0 to 1, as said below
- refill_index: int32 [64, 64], P('fsdp'), may hold values from 0 to 63, each once within a row
Outputs:
- next_states: bfloat16 [4096, 4096], P('fsdp', ('tensor', 'dp'))
Inputs may be any that keep to these rules, and one draw needn't show every extreme that they name: In each aligned block of 512 rows (in row order over all batches) at most 384 rows are running (halted 0), and some block has exactly 384 running rows. Each batch's row of refill_index holds every number of 0 to 63 once.
All inputs are finite; a program needn't handle non-finite values.
Results may differ from a plain program's by a relative error of at most 0.0085.
Values may be sent and summed in bfloat16 or wider, within the bound.
A program may use at most 128 MiB of HBM per device.

v0:
```python
import jax
import jax.numpy as jnp
from jax import lax
from jax.sharding import PartitionSpec as P


norm_eps = 1e-05


def make_body(mesh):
    count_f = mesh.shape["fsdp"]
    count_t = mesh.shape["tensor"]
    count_c = mesh.shape["dp"]
    ring = min(4, max(1, count_f // 2))
    span = count_f // ring
    unit = count_f // (count_t * count_c)

    def send_f(value, step_a, step_b):
        pairs = []
        for a in range(ring):
            for b in range(span):
                pairs.append((a * span + b, ((a + step_a) % ring) * span + (b + step_b) % span))
        return lax.ppermute(value, "fsdp", pairs)

    def send_axis(value, axis, count, step):
        return lax.ppermute(value, axis, [(i, (i + step) % count) for i in range(count)])

    def place(owner):
        t, c = lax.axis_index("tensor"), lax.axis_index("dp")
        block = owner // unit
        block_t, block_c = block // count_c, block % count_c
        near = ((block_c - c) % count_c) * count_t + (block_t - t) % count_t
        return near * unit + owner % unit

    def move_weight(weight, split_axis):
        f = lax.axis_index("fsdp")
        a, b = f // span, f % span
        join_axis = 1 - split_axis
        part = weight.shape[split_axis] // ring
        width = weight.shape[join_axis]
        pieces = [(lax.dynamic_slice_in_dim(weight, a * part, part, split_axis), f)]
        for step in range(1, ring):
            target = (a + step) % ring
            piece = lax.dynamic_slice_in_dim(weight, target * part, part, split_axis)
            pieces.append((send_f(piece, step, 0), ((a - step) % ring) * span + b))
        for piece, owner in list(pieces):
            for step in range(1, span):
                other = (owner // span) * span + (b - step) % span
                pieces.append((send_f(piece, 0, step), other))
        shape = [part, part]
        shape[join_axis] = width * count_f
        whole = jnp.zeros(shape, weight.dtype)
        for piece, owner in pieces:
            whole = lax.dynamic_update_slice_in_dim(whole, piece, place(owner) * width, join_axis)
        return whole

    def block_update(source, norm_gain, gate_weight, up_weight, down_weight):
        capacity, width = source.shape
        features = width * count_t * count_c
        widened = source.astype(jnp.float32)
        mean_square = (
            lax.psum(jnp.sum(widened * widened, axis=-1, keepdims=True), ("tensor", "dp")) / features
        )
        normed = (
            widened * lax.rsqrt(mean_square + norm_eps) * norm_gain.astype(jnp.float32)
        ).astype(jnp.bfloat16)
        gate_full = move_weight(gate_weight, 1)
        up_full = move_weight(up_weight, 1)
        down_full = move_weight(down_weight, 0)
        slots = [normed] + [send_f(normed, k, 0) for k in range(1, ring)]
        columns = [jnp.concatenate(slots, axis=0)]
        for step in range(1, count_t):
            moved = [send_axis(piece, "tensor", count_t, -step) for piece in slots]
            columns.append(jnp.concatenate(moved, axis=0))
        for step in range(1, count_c):
            columns = columns + [send_axis(piece, "dp", count_c, -step) for piece in columns[:count_t]]
        full = jnp.concatenate(columns, axis=1)
        gate_sum = jnp.dot(full, gate_full, preferred_element_type=jnp.float32)
        up_sum = jnp.dot(full, up_full, preferred_element_type=jnp.float32)
        hidden = (jax.nn.silu(gate_sum) * up_sum).astype(jnp.bfloat16)
        half = count_t * width
        total = None
        for slot in list(range(1, ring)) + [0]:
            part = lax.slice_in_dim(hidden, slot * capacity, (slot + 1) * capacity, axis=0)
            products = [
                jnp.dot(
                    part, down_full[:, k * half : (k + 1) * half], preferred_element_type=jnp.float32
                ).astype(jnp.bfloat16)
                for k in range(count_c)
            ]
            own = products[0].astype(jnp.float32)
            for step in range(1, count_c):
                own = own + send_axis(products[step], "dp", count_c, step).astype(jnp.float32)
            own = own.astype(jnp.bfloat16)
            mine = own[:, :width].astype(jnp.float32)
            for step in range(1, count_t):
                away = own[:, step * width : (step + 1) * width]
                moved = send_axis(away, "tensor", count_t, step)
                mine = mine + moved.astype(jnp.float32)
            if slot:
                mine = send_f(mine.astype(jnp.bfloat16), -slot, 0).astype(jnp.float32)
            total = mine if total is None else total + mine
        return total

    def body(states, fresh_rows, norm_gain, gate_weight, up_weight, down_weight, halted, refill_index):
        row_count = states.shape[0]
        running = halted.reshape(row_count) == 0
        capacity = row_count * 3 // 4
        slot_of = jnp.cumsum(running.astype(jnp.int32)) - 1
        slot_ids = lax.iota(jnp.int32, capacity)
        picker = ((slot_of[None, :] == slot_ids[:, None]) & running[None, :]).astype(jnp.bfloat16)
        source = jnp.dot(picker, states, preferred_element_type=jnp.float32).astype(jnp.bfloat16)
        compact = block_update(source, norm_gain, gate_weight, up_weight, down_weight)
        update = jnp.take(compact, jnp.clip(slot_of, 0, capacity - 1), axis=0)
        block_total = refill_index.shape[0]
        batch_len = refill_index.shape[1]
        fresh_blocks = fresh_rows.reshape(block_total, batch_len, fresh_rows.shape[1])
        refilled = jax.vmap(lambda block_rows, pick_index: block_rows[pick_index])(
            fresh_blocks, refill_index
        )
        refilled = refilled.reshape(row_count, fresh_rows.shape[1])
        computed = (states.astype(jnp.float32) + update).astype(jnp.bfloat16)
        return jnp.where(running[:, None], computed, refilled)

    return body


def solution(mesh):
    in_specs = (
        P("fsdp", ("tensor", "dp")),
        P("fsdp", ("tensor", "dp")),
        P(("tensor", "dp")),
        P("fsdp", ("tensor", "dp")),
        P("fsdp", ("tensor", "dp")),
        P(("tensor", "dp"), "fsdp"),
        P("fsdp", None),
        P("fsdp", None),
    )
    out_specs = P("fsdp", ("tensor", "dp"))
    body = make_body(mesh)

    return jax.shard_map(body, mesh=mesh, in_specs=in_specs, out_specs=out_specs, check_vma=False)
```

profile of v0, /device:TPU:0, one launch (start us, length us, event | category | flops | bytes accessed | tf_op | source)
XLA Modules:
  0.0 491.3 jit_solution(16975148767274368436)
XLA Ops:
  4.1 8.4 %psum.7 = f32[384,1]{0,1:T(1,128)S(1)} all-reduce(f32[384,1]{0,1:T(1,128)S(1)} %broadcast_in_dim.34), channel_id=1, replica_groups=mesh['fsdp'=8,'tensor'=2,'dp'=2] {'tensor','dp'}, use_global_device_ids=true, to_apply=%region_3.4 | all-reduce | flops 384 | bytes 3072 | tf_op jit(solution)/shard_map/psum | solution.py:62
  22.2 24.3 %collective-permute-done.23 = bf16[512,512]{1,0:T(8,128)(2,1)S(1)} collective-permute-done((bf16[512,512]{1,0:T(8,128)(2,1)S(1)}, bf16[512,512]{1,0:T(8,128)(2,1)S(1)}, u32[]{:S(2)}, u32[]{:S(2)}) %collective-permute-start.23) | collective-permute-done | bytes 524320 | tf_op jit(solution)/shard_map/ppermute | solution.py:23
  46.6 70.7 %collective-permute-done.24 = bf16[512,512]{1,0:T(8,128)(2,1)S(1)} collective-permute-done((bf16[512,512]{1,0:T(8,128)(2,1)S(1)}, bf16[512,512]{1,0:T(8,128)(2,1)S(1)}, u32[]{:S(2)}, u32[]{:S(2)}) %collective-permute-start.24) | collective-permute-done | bytes 524320 | tf_op jit(solution)/shard_map/ppermute | solution.py:23
  128.6 9.1 %collective-permute-done.3 = bf16[384,1024]{1,0:T(8,128)(2,1)S(1)} collective-permute-done((bf16[384,1024]{1,0:T(8,128)(2,1)S(1)}, bf16[384,1024]{1,0:T(8,128)(2,1)S(1)}, u32[]{:S(2)}, u32[]{:S(2)}) %collective-permute-start.3) | collective-permute-done | bytes 786464 | tf_op jit(solution)/shard_map/ppermute | solution.py:26
  137.7 9.8 %collective-permute-start.9 = (bf16[512,512]{1,0:T(8,128)(2,1)S(1)}, bf16[512,512]{1,0:T(8,128)(2,1)S(1)}, u32[]{:S(2)}, u32[]{:S(2)}) collective-permute-start(bf16[512,512]{1,0:T(8,128)(2,1)S(1)} %get-tuple-element.16), channel_id=1, source_target_pairs={{0,8},{4,12},{8,16},{12,20},{16,24},{20,28},{24,0},{28,4},{1,9},{5... | collective-permute-start | bytes 1572872 | tf_op jit(solution)/shard_map/ppermute | solution.py:23
  147.5 7.0 %collective-permute-done.4 = bf16[384,1024]{1,0:T(8,128)(2,1)S(1)} collective-permute-done((bf16[384,1024]{1,0:T(8,128)(2,1)S(1)}, bf16[384,1024]{1,0:T(8,128)(2,1)S(1)}, u32[]{:S(2)}, u32[]{:S(2)}) %collective-permute-start.4) | collective-permute-done | bytes 786464 | tf_op jit(solution)/shard_map/ppermute | solution.py:26
  156.4 15.0 %collective-permute-done.5 = bf16[384,1024]{1,0:T(8,128)(2,1)S(1)} collective-permute-done((bf16[384,1024]{1,0:T(8,128)(2,1)S(1)}, bf16[384,1024]{1,0:T(8,128)(2,1)S(1)}, u32[]{:S(2)}, u32[]{:S(2)}) %collective-permute-start.5) | collective-permute-done | bytes 786464 | tf_op jit(solution)/shard_map/ppermute | solution.py:26
  171.4 12.6 %collective-permute-start.11 = (bf16[512,512]{1,0:T(8,128)(2,1)S(1)}, bf16[512,512]{1,0:T(8,128)(2,1)S(1)}, u32[]{:S(2)}, u32[]{:S(2)}) collective-permute-start(bf16[512,512]{1,0:T(8,128)(2,1)S(1)} %get-tuple-element.15), channel_id=1, source_target_pairs={{0,24},{4,28},{8,0},{12,4},{16,8},{20,12},{24,16},{28,20},{1,25},{... | collective-permute-start | bytes 1572872 | tf_op jit(solution)/shard_map/ppermute | solution.py:23
  187.2 8.5 %collective-permute-start.16 = (bf16[512,512]{1,0:T(8,128)(2,1)}, bf16[512,512]{1,0:T(8,128)(2,1)}, u32[]{:S(2)}, u32[]{:S(2)}) collective-permute-start(bf16[512,512]{1,0:T(8,128)(2,1)} %get-tuple-element.21), channel_id=1, source_target_pairs={{0,8},{4,12},{8,16},{12,20},{16,24},{20,28},{24,0},{28,4},{1,9},{5... | collective-permute-start | bytes 1572872 | tf_op jit(solution)/shard_map/ppermute | solution.py:23
  202.7 9.0 %collective-permute-done.16 = bf16[512,512]{1,0:T(8,128)(2,1)} collective-permute-done((bf16[512,512]{1,0:T(8,128)(2,1)}, bf16[512,512]{1,0:T(8,128)(2,1)}, u32[]{:S(2)}, u32[]{:S(2)}) %collective-permute-start.16) | collective-permute-done | bytes 524320 | tf_op jit(solution)/shard_map/ppermute | solution.py:23
  219.2 12.0 %collective-permute-done.17 = bf16[512,512]{1,0:T(8,128)(2,1)} collective-permute-done((bf16[512,512]{1,0:T(8,128)(2,1)}, bf16[512,512]{1,0:T(8,128)(2,1)}, u32[]{:S(2)}, u32[]{:S(2)}) %collective-permute-start.17) | collective-permute-done | bytes 524320 | tf_op jit(solution)/shard_map/ppermute | solution.py:23
  240.3 5.8 %collective-permute-done.27 = bf16[512,512]{1,0:T(8,128)(2,1)S(1)} collective-permute-done((bf16[512,512]{1,0:T(8,128)(2,1)S(1)}, bf16[512,512]{1,0:T(8,128)(2,1)S(1)}, u32[]{:S(2)}, u32[]{:S(2)}) %collective-permute-start.27) | collective-permute-done | bytes 524320 | tf_op jit(solution)/shard_map/ppermute | solution.py:23
  248.7 8.6 %collective-permute-done.28 = bf16[512,512]{1,0:T(8,128)(2,1)S(1)} collective-permute-done((bf16[512,512]{1,0:T(8,128)(2,1)S(1)}, bf16[512,512]{1,0:T(8,128)(2,1)S(1)}, u32[]{:S(2)}, u32[]{:S(2)}) %collective-permute-start.28) | collective-permute-done | bytes 524320 | tf_op jit(solution)/shard_map/ppermute | solution.py:23
  259.9 8.6 %collective-permute-done.29 = bf16[512,512]{1,0:T(8,128)(2,1)S(1)} collective-permute-done((bf16[512,512]{1,0:T(8,128)(2,1)S(1)}, bf16[512,512]{1,0:T(8,128)(2,1)S(1)}, u32[]{:S(2)}, u32[]{:S(2)}) %collective-permute-start.29) | collective-permute-done | bytes 524320 | tf_op jit(solution)/shard_map/ppermute | solution.py:23
  271.3 8.5 %collective-permute-done.13 = bf16[512,512]{1,0:T(8,128)(2,1)S(1)} collective-permute-done((bf16[512,512]{1,0:T(8,128)(2,1)S(1)}, bf16[512,512]{1,0:T(8,128)(2,1)S(1)}, u32[]{:S(2)}, u32[]{:S(2)}) %collective-permute-start.13) | collective-permute-done | bytes 524320 | tf_op jit(solution)/shard_map/ppermute | solution.py:23
  282.2 8.8 %collective-permute-done.14 = bf16[512,512]{1,0:T(8,128)(2,1)S(1)} collective-permute-done((bf16[512,512]{1,0:T(8,128)(2,1)S(1)}, bf16[512,512]{1,0:T(8,128)(2,1)S(1)}, u32[]{:S(2)}, u32[]{:S(2)}) %collective-permute-start.14) | collective-permute-done | bytes 524320 | tf_op jit(solution)/shard_map/ppermute | solution.py:23
  292.6 9.6 %collective-permute-done.15 = bf16[512,512]{1,0:T(8,128)(2,1)S(1)} collective-permute-done((bf16[512,512]{1,0:T(8,128)(2,1)S(1)}, bf16[512,512]{1,0:T(8,128)(2,1)S(1)}, u32[]{:S(2)}, u32[]{:S(2)}) %collective-permute-start.15) | collective-permute-done | bytes 524320 | tf_op jit(solution)/shard_map/ppermute | solution.py:23
  305.5 8.0 %collective-permute-done.20 = bf16[512,512]{1,0:T(8,128)(2,1)S(1)} collective-permute-done((bf16[512,512]{1,0:T(8,128)(2,1)}, bf16[512,512]{1,0:T(8,128)(2,1)S(1)}, u32[]{:S(2)}, u32[]{:S(2)}) %collective-permute-start.20) | collective-permute-done | bytes 524320 | tf_op jit(solution)/shard_map/ppermute | solution.py:23
  313.5 11.2 %collective-permute-done.21 = bf16[512,512]{1,0:T(8,128)(2,1)S(1)} collective-permute-done((bf16[512,512]{1,0:T(8,128)(2,1)}, bf16[512,512]{1,0:T(8,128)(2,1)S(1)}, u32[]{:S(2)}, u32[]{:S(2)}) %collective-permute-start.21) | collective-permute-done | bytes 524320 | tf_op jit(solution)/shard_map/ppermute | solution.py:23
  324.7 10.3 %collective-permute-done.22 = bf16[512,512]{1,0:T(8,128)(2,1)S(1)} collective-permute-done((bf16[512,512]{1,0:T(8,128)(2,1)}, bf16[512,512]{1,0:T(8,128)(2,1)S(1)}, u32[]{:S(2)}, u32[]{:S(2)}) %collective-permute-start.22) | collective-permute-done | bytes 524320 | tf_op jit(solution)/shard_map/ppermute | solution.py:23
  335.1 28.5 %pad_maximum_fusion = bf16[1536,4096]{1,0:T(8,128)(2,1)S(1)} fusion(bf16[1536,1024]{1,0:T(8,128)(2,1)} %collective-permute-done.8, bf16[1536,1024]{1,0:T(8,128)(2,1)} %collective-permute-done.7, bf16[1536,1024]{1,0:T(8,128)(2,1)} %constant_dynamic-update-slice_fusion.24, bf16[384,1024]{1,0:T(8,128)(2,1)S(1)} %copy-done.9, ...), kind=kLoop, calls=%fused_computation.2 | loop fusion | flops 88080384 | bytes 25165824 | tf_op jit(solution)/shard_map/concatenate | solution.py:77
  363.6 6.7 %fusion.32 = f32[1536,512]{1,0:T(8,128)S(1)} fusion(bf16[1536,4096]{1,0:T(8,128)(2,1)S(1)} %pad_maximum_fusion, bf16[4096,512]{1,0:T(8,128)(2,1)S(1)} %copy-done.7), kind=kOutput, calls=%fused_computation.105 | convolution fusion | flops 6442450944 | bytes 19922944 | tf_op jit(solution)/shard_map/dot_general | solution.py:78
  370.3 7.6 %multiply_convert_fusion = bf16[1536,512]{1,0:T(8,128)(2,1)S(1)} fusion(f32[1536,512]{1,0:T(8,128)S(1)} %fusion.32, bf16[1536,4096]{1,0:T(8,128)(2,1)S(1)} %pad_maximum_fusion, bf16[4096,512]{1,0:T(8,128)(2,1)S(1)} %constant_dynamic-update-slice_fusion.8), kind=kOutput, calls=%fused_computation.8 | convolution fusion | flops 6447169536 | bytes 21495808 | tf_op jit(solution)/shard_map/dot_general | solution.py:79
  394.5 13.9 %collective-permute-done.37 = bf16[384,1024]{1,0:T(8,128)(2,1)S(1)} collective-permute-done((bf16[384,1024]{1,0:T(8,128)(2,1)S(1)}, bf16[384,1024]{1,0:T(8,128)(2,1)S(1)}, u32[]{:S(2)}, u32[]{:S(2)}) %collective-permute-start.37) | collective-permute-done | bytes 786464 | tf_op jit(solution)/shard_map/ppermute | solution.py:26
  408.8 6.3 %collective-permute-start.38 = (bf16[384,1024]{1,0:T(8,128)(2,1)S(1)}, bf16[384,1024]{1,0:T(8,128)(2,1)}, u32[]{:S(2)}, u32[]{:S(2)}) collective-permute-start(bf16[384,1024]{1,0:T(8,128)(2,1)S(1)} %add_convert_fusion.5), channel_id=1, source_target_pairs={{0,8},{4,12},{8,16},{12,20},{16,24},{20,28},{24,0},{28,4},{1,9},{5... | collective-permute-start | bytes 2359304 | tf_op jit(solution)/shard_map/ppermute | solution.py:23
  415.0 10.3 %collective-permute-done.34 = bf16[384,1024]{1,0:T(8,128)(2,1)S(1)} collective-permute-done((bf16[384,1024]{1,0:T(8,128)(2,1)S(1)}, bf16[384,1024]{1,0:T(8,128)(2,1)S(1)}, u32[]{:S(2)}, u32[]{:S(2)}) %collective-permute-start.34) | collective-permute-done | bytes 786464 | tf_op jit(solution)/shard_map/ppermute | solution.py:26
  426.5 5.2 %collective-permute-start.35 = (bf16[384,1024]{1,0:T(8,128)(2,1)}, bf16[384,1024]{1,0:T(8,128)(2,1)}, u32[]{:S(2)}, u32[]{:S(2)}) collective-permute-start(bf16[384,1024]{1,0:T(8,128)(2,1)} %add_convert_fusion.6), channel_id=1, source_target_pairs={{0,16},{4,20},{8,24},{12,28},{16,0},{20,4},{24,8},{28,12},{1,17},{... | collective-permute-start | bytes 2359304 | tf_op jit(solution)/shard_map/ppermute | solution.py:23
  431.6 10.5 %collective-permute-done.31 = bf16[384,1024]{1,0:T(8,128)(2,1)S(1)} collective-permute-done((bf16[384,1024]{1,0:T(8,128)(2,1)S(1)}, bf16[384,1024]{1,0:T(8,128)(2,1)S(1)}, u32[]{:S(2)}, u32[]{:S(2)}) %collective-permute-start.31) | collective-permute-done | bytes 786464 | tf_op jit(solution)/shard_map/ppermute | solution.py:26
  443.4 8.0 %collective-permute-start.32 = (bf16[384,1024]{1,0:T(8,128)(2,1)}, bf16[384,1024]{1,0:T(8,128)(2,1)}, u32[]{:S(2)}, u32[]{:S(2)}) collective-permute-start(bf16[384,1024]{1,0:T(8,128)(2,1)} %add_convert_fusion.7), channel_id=1, source_target_pairs={{0,24},{4,28},{8,0},{12,4},{16,8},{20,12},{24,16},{28,20},{1,25},{... | collective-permute-start | bytes 2359304 | tf_op jit(solution)/shard_map/ppermute | solution.py:23
  451.5 8.1 %gather_fusion.1 = bf16[512,1024]{1,0:T(8,128)(2,1)} fusion(bf16[8,64,1024]{2,1,0:T(8,128)(2,1)S(1)} %bitcast.17, s32[512]{0:T(512)S(1)} %reshape.108), kind=kCustom, calls=%fused_computation.1 | custom fusion | bytes 2101248 | tf_op jit(solution)/shard_map/vmap()/gather | solution.py:118
  459.7 7.7 %collective-permute-done.35 = bf16[384,1024]{1,0:T(8,128)(2,1)} collective-permute-done((bf16[384,1024]{1,0:T(8,128)(2,1)}, bf16[384,1024]{1,0:T(8,128)(2,1)}, u32[]{:S(2)}, u32[]{:S(2)}) %collective-permute-start.35) | collective-permute-done | bytes 786464 | tf_op jit(solution)/shard_map/ppermute | solution.py:23
  467.3 14.5 %collective-permute-done.32 = bf16[384,1024]{1,0:T(8,128)(2,1)} collective-permute-done((bf16[384,1024]{1,0:T(8,128)(2,1)}, bf16[384,1024]{1,0:T(8,128)(2,1)}, u32[]{:S(2)}, u32[]{:S(2)}) %collective-permute-start.32) | collective-permute-done | bytes 786464 | tf_op jit(solution)/shard_map/ppermute | solution.py:23
  (183 shorter events, 96.9 us)
Async XLA Ops:
  12.8 106.0 %collective-permute-start = (bf16[384,1024]{1,0:T(8,128)(2,1)S(1)}, bf16[384,1024]{1,0:T(8,128)(2,1)S(1)}, u32[]{:S(2)}, u32[]{:S(2)}) collective-permute-start(bf16[384,1024]{1,0:T(8,128)(2,1)S(1)} %fusion.2), channel_id=1, source_target_pairs={{0,8},{4,12},{8,16},{12,20},{16,24},{20,28},{24,0},{28,4},{1,9},{5... | collective-permute-start | bytes 2359304 | tf_op jit(solution)/shard_map/ppermute | solution.py:23
  16.3 30.2 %collective-permute-start.23 = (bf16[512,512]{1,0:T(8,128)(2,1)S(1)}, bf16[512,512]{1,0:T(8,128)(2,1)S(1)}, u32[]{:S(2)}, u32[]{:S(2)}) collective-permute-start(bf16[512,512]{1,0:T(8,128)(2,1)S(1)} %get-tuple-element.26), channel_id=1, source_target_pairs={{0,8},{4,12},{8,16},{12,20},{16,24},{20,28},{24,0},{28,4},{1,9},{5... | collective-permute-start | bytes 1572872 | tf_op jit(solution)/shard_map/ppermute | solution.py:23
  17.9 102.8 %collective-permute-start.1 = (bf16[384,1024]{1,0:T(8,128)(2,1)S(1)}, bf16[384,1024]{1,0:T(8,128)(2,1)S(1)}, u32[]{:S(2)}, u32[]{:S(2)}) collective-permute-start(bf16[384,1024]{1,0:T(8,128)(2,1)S(1)} %fusion.2), channel_id=1, source_target_pairs={{0,16},{4,20},{8,24},{12,28},{16,0},{20,4},{24,8},{28,12},{1,17},{... | collective-permute-start | bytes 2359304 | tf_op jit(solution)/shard_map/ppermute | solution.py:23
  19.2 103.1 %collective-permute-start.2 = (bf16[384,1024]{1,0:T(8,128)(2,1)S(1)}, bf16[384,1024]{1,0:T(8,128)(2,1)S(1)}, u32[]{:S(2)}, u32[]{:S(2)}) collective-permute-start(bf16[384,1024]{1,0:T(8,128)(2,1)S(1)} %fusion.2), channel_id=1, source_target_pairs={{0,24},{4,28},{8,0},{12,4},{16,8},{20,12},{24,16},{28,20},{1,25},{... | collective-permute-start | bytes 2359304 | tf_op jit(solution)/shard_map/ppermute | solution.py:23
  21.9 95.4 %collective-permute-start.24 = (bf16[512,512]{1,0:T(8,128)(2,1)S(1)}, bf16[512,512]{1,0:T(8,128)(2,1)S(1)}, u32[]{:S(2)}, u32[]{:S(2)}) collective-permute-start(bf16[512,512]{1,0:T(8,128)(2,1)S(1)} %get-tuple-element.29), channel_id=1, source_target_pairs={{0,16},{4,20},{8,24},{12,28},{16,0},{20,4},{24,8},{28,12},{1,17},{... | collective-permute-start | bytes 1572872 | tf_op jit(solution)/shard_map/ppermute | solution.py:23
  46.5 78.7 %collective-permute-start.25 = (bf16[512,512]{1,0:T(8,128)(2,1)S(1)}, bf16[512,512]{1,0:T(8,128)(2,1)S(1)}, u32[]{:S(2)}, u32[]{:S(2)}) collective-permute-start(bf16[512,512]{1,0:T(8,128)(2,1)S(1)} %get-tuple-element.25), channel_id=1, source_target_pairs={{0,24},{4,28},{8,0},{12,4},{16,8},{20,12},{24,16},{28,20},{1,25},{... | collective-permute-start | bytes 1572872 | tf_op jit(solution)/shard_map/ppermute | solution.py:23
  118.8 35.7 %collective-permute-start.4 = (bf16[384,1024]{1,0:T(8,128)(2,1)S(1)}, bf16[384,1024]{1,0:T(8,128)(2,1)S(1)}, u32[]{:S(2)}, u32[]{:S(2)}) collective-permute-start(bf16[384,1024]{1,0:T(8,128)(2,1)S(1)} %collective-permute-done), channel_id=1, source_target_pairs={{0,2},{2,0},{1,3},{3,1},{4,6},{6,4},{5,7},{7,5},{8,10},{10,8},{9,1... | collective-permute-start | bytes 2359304 | tf_op jit(solution)/shard_map/ppermute | solution.py:26
  120.7 50.7 %collective-permute-start.5 = (bf16[384,1024]{1,0:T(8,128)(2,1)S(1)}, bf16[384,1024]{1,0:T(8,128)(2,1)S(1)}, u32[]{:S(2)}, u32[]{:S(2)}) collective-permute-start(bf16[384,1024]{1,0:T(8,128)(2,1)S(1)} %collective-permute-done.1), channel_id=1, source_target_pairs={{0,2},{2,0},{1,3},{3,1},{4,6},{6,4},{5,7},{7,5},{8,10},{10,8},{9,1... | collective-permute-start | bytes 2359304 | tf_op jit(solution)/shard_map/ppermute | solution.py:26
  122.3 64.9 %collective-permute-start.6 = (bf16[384,1024]{1,0:T(8,128)(2,1)S(1)}, bf16[384,1024]{1,0:T(8,128)(2,1)S(1)}, u32[]{:S(2)}, u32[]{:S(2)}) collective-permute-start(bf16[384,1024]{1,0:T(8,128)(2,1)S(1)} %collective-permute-done.2), channel_id=1, source_target_pairs={{0,2},{2,0},{1,3},{3,1},{4,6},{6,4},{5,7},{7,5},{8,10},{10,8},{9,1... | collective-permute-start | bytes 2359304 | tf_op jit(solution)/shard_map/ppermute | solution.py:26
  125.2 59.9 %collective-permute-start.26 = (bf16[512,512]{1,0:T(8,128)(2,1)S(1)}, bf16[512,512]{1,0:T(8,128)(2,1)S(1)}, u32[]{:S(2)}, u32[]{:S(2)}) collective-permute-start(bf16[512,512]{1,0:T(8,128)(2,1)S(1)} %get-tuple-element.28), channel_id=1, source_target_pairs={{0,4},{4,0},{8,12},{12,8},{16,20},{20,16},{24,28},{28,24},{1,5},{5... | collective-permute-start | bytes 1572872 | tf_op jit(solution)/shard_map/ppermute | solution.py:23
  137.7 59.1 %collective-permute-start.9 = (bf16[512,512]{1,0:T(8,128)(2,1)S(1)}, bf16[512,512]{1,0:T(8,128)(2,1)S(1)}, u32[]{:S(2)}, u32[]{:S(2)}) collective-permute-start(bf16[512,512]{1,0:T(8,128)(2,1)S(1)} %get-tuple-element.16), channel_id=1, source_target_pairs={{0,8},{4,12},{8,16},{12,20},{16,24},{20,28},{24,0},{28,4},{1,9},{5... | collective-permute-start | bytes 1572872 | tf_op jit(solution)/shard_map/ppermute | solution.py:23
  154.6 42.2 %collective-permute-start.10 = (bf16[512,512]{1,0:T(8,128)(2,1)S(1)}, bf16[512,512]{1,0:T(8,128)(2,1)S(1)}, u32[]{:S(2)}, u32[]{:S(2)}) collective-permute-start(bf16[512,512]{1,0:T(8,128)(2,1)S(1)} %get-tuple-element.19), channel_id=1, source_target_pairs={{0,16},{4,20},{8,24},{12,28},{16,0},{20,4},{24,8},{28,12},{1,17},{... | collective-permute-start | bytes 1572872 | tf_op jit(solution)/shard_map/ppermute | solution.py:23
  171.4 25.9 %collective-permute-start.11 = (bf16[512,512]{1,0:T(8,128)(2,1)S(1)}, bf16[512,512]{1,0:T(8,128)(2,1)S(1)}, u32[]{:S(2)}, u32[]{:S(2)}) collective-permute-start(bf16[512,512]{1,0:T(8,128)(2,1)S(1)} %get-tuple-element.15), channel_id=1, source_target_pairs={{0,24},{4,28},{8,0},{12,4},{16,8},{20,12},{24,16},{28,20},{1,25},{... | collective-permute-start | bytes 1572872 | tf_op jit(solution)/shard_map/ppermute | solution.py:23
  187.2 24.5 %collective-permute-start.16 = (bf16[512,512]{1,0:T(8,128)(2,1)}, bf16[512,512]{1,0:T(8,128)(2,1)}, u32[]{:S(2)}, u32[]{:S(2)}) collective-permute-start(bf16[512,512]{1,0:T(8,128)(2,1)} %get-tuple-element.21), channel_id=1, source_target_pairs={{0,8},{4,12},{8,16},{12,20},{16,24},{20,28},{24,0},{28,4},{1,9},{5... | collective-permute-start | bytes 1572872 | tf_op jit(solution)/shard_map/ppermute | solution.py:23
  196.8 138.3 %collective-permute-start.7 = (bf16[1536,1024]{1,0:T(8,128)(2,1)}, bf16[1536,1024]{1,0:T(8,128)(2,1)}, u32[]{:S(2)}, u32[]{:S(2)}) collective-permute-start(bf16[1536,1024]{1,0:T(8,128)(2,1)} %pad_maximum_fusion.1), channel_id=1, source_target_pairs={{0,1},{1,0},{2,3},{3,2},{4,5},{5,4},{6,7},{7,6},{8,9},{9,8},{10,11... | collective-permute-start | bytes 9437192 | tf_op jit(solution)/shard_map/ppermute | solution.py:26
  196.8 138.3 %collective-permute-start.8 = (bf16[1536,1024]{1,0:T(8,128)(2,1)}, bf16[1536,1024]{1,0:T(8,128)(2,1)}, u32[]{:S(2)}, u32[]{:S(2)}) collective-permute-start(bf16[1536,1024]{1,0:T(8,128)(2,1)} %constant_dynamic-update-slice_fusion.24), channel_id=1, source_target_pairs={{0,1},{1,0},{2,3},{3,2},{4,5},{5,4},{6,7},{7,6},{8,9},{9,8},{10,11... | collective-permute-start | bytes 9437192 | tf_op jit(solution)/shard_map/ppermute | solution.py:26
  198.4 32.8 %collective-permute-start.17 = (bf16[512,512]{1,0:T(8,128)(2,1)}, bf16[512,512]{1,0:T(8,128)(2,1)}, u32[]{:S(2)}, u32[]{:S(2)}) collective-permute-start(bf16[512,512]{1,0:T(8,128)(2,1)} %get-tuple-element.24), channel_id=1, source_target_pairs={{0,16},{4,20},{8,24},{12,28},{16,0},{20,4},{24,8},{28,12},{1,17},{... | collective-permute-start | bytes 1572872 | tf_op jit(solution)/shard_map/ppermute | solution.py:23
  201.8 31.8 %collective-permute-start.18 = (bf16[512,512]{1,0:T(8,128)(2,1)}, bf16[512,512]{1,0:T(8,128)(2,1)}, u32[]{:S(2)}, u32[]{:S(2)}) collective-permute-start(bf16[512,512]{1,0:T(8,128)(2,1)} %get-tuple-element.20), channel_id=1, source_target_pairs={{0,24},{4,28},{8,0},{12,4},{16,8},{20,12},{24,16},{28,20},{1,25},{... | collective-permute-start | bytes 1572872 | tf_op jit(solution)/shard_map/ppermute | solution.py:23
  233.6 23.6 %collective-permute-start.28 = (bf16[512,512]{1,0:T(8,128)(2,1)S(1)}, bf16[512,512]{1,0:T(8,128)(2,1)S(1)}, u32[]{:S(2)}, u32[]{:S(2)}) collective-permute-start(bf16[512,512]{1,0:T(8,128)(2,1)S(1)} %copy-done.18), channel_id=1, source_target_pairs={{0,4},{4,0},{8,12},{12,8},{16,20},{20,16},{24,28},{28,24},{1,5},{5... | collective-permute-start | bytes 1572872 | tf_op jit(solution)/shard_map/ppermute | solution.py:23
  235.0 33.5 %collective-permute-start.29 = (bf16[512,512]{1,0:T(8,128)(2,1)S(1)}, bf16[512,512]{1,0:T(8,128)(2,1)S(1)}, u32[]{:S(2)}, u32[]{:S(2)}) collective-permute-start(bf16[512,512]{1,0:T(8,128)(2,1)S(1)} %copy-done.14), channel_id=1, source_target_pairs={{0,4},{4,0},{8,12},{12,8},{16,20},{20,16},{24,28},{28,24},{1,5},{5... | collective-permute-start | bytes 1572872 | tf_op jit(solution)/shard_map/ppermute | solution.py:23
  246.0 33.7 %collective-permute-start.13 = (bf16[512,512]{1,0:T(8,128)(2,1)S(1)}, bf16[512,512]{1,0:T(8,128)(2,1)S(1)}, u32[]{:S(2)}, u32[]{:S(2)}) collective-permute-start(bf16[512,512]{1,0:T(8,128)(2,1)S(1)} %copy-done.24), channel_id=1, source_target_pairs={{0,4},{4,0},{8,12},{12,8},{16,20},{20,16},{24,28},{28,24},{1,5},{5... | collective-permute-start | bytes 1572872 | tf_op jit(solution)/shard_map/ppermute | solution.py:23
  257.3 33.7 %collective-permute-start.14 = (bf16[512,512]{1,0:T(8,128)(2,1)S(1)}, bf16[512,512]{1,0:T(8,128)(2,1)S(1)}, u32[]{:S(2)}, u32[]{:S(2)}) collective-permute-start(bf16[512,512]{1,0:T(8,128)(2,1)S(1)} %copy-done.20), channel_id=1, source_target_pairs={{0,4},{4,0},{8,12},{12,8},{16,20},{20,16},{24,28},{28,24},{1,5},{5... | collective-permute-start | bytes 1572872 | tf_op jit(solution)/shard_map/ppermute | solution.py:23
  268.5 33.7 %collective-permute-start.15 = (bf16[512,512]{1,0:T(8,128)(2,1)S(1)}, bf16[512,512]{1,0:T(8,128)(2,1)S(1)}, u32[]{:S(2)}, u32[]{:S(2)}) collective-permute-start(bf16[512,512]{1,0:T(8,128)(2,1)S(1)} %copy-done.22), channel_id=1, source_target_pairs={{0,4},{4,0},{8,12},{12,8},{16,20},{20,16},{24,28},{28,24},{1,5},{5... | collective-permute-start | bytes 1572872 | tf_op jit(solution)/shard_map/ppermute | solution.py:23
  279.7 33.7 %collective-permute-start.20 = (bf16[512,512]{1,0:T(8,128)(2,1)}, bf16[512,512]{1,0:T(8,128)(2,1)S(1)}, u32[]{:S(2)}, u32[]{:S(2)}) collective-permute-start(bf16[512,512]{1,0:T(8,128)(2,1)} %collective-permute-done.16), channel_id=1, source_target_pairs={{0,4},{4,0},{8,12},{12,8},{16,20},{20,16},{24,28},{28,24},{1,5},{5... | collective-permute-start | bytes 1572872 | tf_op jit(solution)/shard_map/ppermute | solution.py:23
  291.0 33.7 %collective-permute-start.21 = (bf16[512,512]{1,0:T(8,128)(2,1)}, bf16[512,512]{1,0:T(8,128)(2,1)S(1)}, u32[]{:S(2)}, u32[]{:S(2)}) collective-permute-start(bf16[512,512]{1,0:T(8,128)(2,1)} %collective-permute-done.17), channel_id=1, source_target_pairs={{0,4},{4,0},{8,12},{12,8},{16,20},{20,16},{24,28},{28,24},{1,5},{5... | collective-permute-start | bytes 1572872 | tf_op jit(solution)/shard_map/ppermute | solution.py:23
  302.2 32.8 %collective-permute-start.22 = (bf16[512,512]{1,0:T(8,128)(2,1)}, bf16[512,512]{1,0:T(8,128)(2,1)S(1)}, u32[]{:S(2)}, u32[]{:S(2)}) collective-permute-start(bf16[512,512]{1,0:T(8,128)(2,1)} %collective-permute-done.18), channel_id=1, source_target_pairs={{0,4},{4,0},{8,12},{12,8},{16,20},{20,16},{24,28},{28,24},{1,5},{5... | collective-permute-start | bytes 1572872 | tf_op jit(solution)/shard_map/ppermute | solution.py:23
  390.7 34.6 %collective-permute-start.34 = (bf16[384,1024]{1,0:T(8,128)(2,1)S(1)}, bf16[384,1024]{1,0:T(8,128)(2,1)S(1)}, u32[]{:S(2)}, u32[]{:S(2)}) collective-permute-start(bf16[384,1024]{1,0:T(8,128)(2,1)S(1)} %slice.82), channel_id=1, source_target_pairs={{0,2},{2,0},{1,3},{3,1},{4,6},{6,4},{5,7},{7,5},{8,10},{10,8},{9,1... | collective-permute-start | bytes 2359304 | tf_op jit(solution)/shard_map/ppermute | solution.py:26
  391.6 50.5 %collective-permute-start.31 = (bf16[384,1024]{1,0:T(8,128)(2,1)S(1)}, bf16[384,1024]{1,0:T(8,128)(2,1)S(1)}, u32[]{:S(2)}, u32[]{:S(2)}) collective-permute-start(bf16[384,1024]{1,0:T(8,128)(2,1)S(1)} %slice.79), channel_id=1, source_target_pairs={{0,2},{2,0},{1,3},{3,1},{4,6},{6,4},{5,7},{7,5},{8,10},{10,8},{9,1... | collective-permute-start | bytes 2359304 | tf_op jit(solution)/shard_map/ppermute | solution.py:26
  394.4 65.3 %collective-permute-start.40 = (bf16[384,1024]{1,0:T(8,128)(2,1)S(1)}, bf16[384,1024]{1,0:T(8,128)(2,1)}, u32[]{:S(2)}, u32[]{:S(2)}) collective-permute-start(bf16[384,1024]{1,0:T(8,128)(2,1)S(1)} %slice.88), channel_id=1, source_target_pairs={{0,2},{2,0},{1,3},{3,1},{4,6},{6,4},{5,7},{7,5},{8,10},{10,8},{9,1... | collective-permute-start | bytes 2359304 | tf_op jit(solution)/shard_map/ppermute | solution.py:26
  408.8 50.9 %collective-permute-start.38 = (bf16[384,1024]{1,0:T(8,128)(2,1)S(1)}, bf16[384,1024]{1,0:T(8,128)(2,1)}, u32[]{:S(2)}, u32[]{:S(2)}) collective-permute-start(bf16[384,1024]{1,0:T(8,128)(2,1)S(1)} %add_convert_fusion.5), channel_id=1, source_target_pairs={{0,8},{4,12},{8,16},{12,20},{16,24},{20,28},{24,0},{28,4},{1,9},{5... | collective-permute-start | bytes 2359304 | tf_op jit(solution)/shard_map/ppermute | solution.py:23
  426.5 40.9 %collective-permute-start.35 = (bf16[384,1024]{1,0:T(8,128)(2,1)}, bf16[384,1024]{1,0:T(8,128)(2,1)}, u32[]{:S(2)}, u32[]{:S(2)}) collective-permute-start(bf16[384,1024]{1,0:T(8,128)(2,1)} %add_convert_fusion.6), channel_id=1, source_target_pairs={{0,16},{4,20},{8,24},{12,28},{16,0},{20,4},{24,8},{28,12},{1,17},{... | collective-permute-start | bytes 2359304 | tf_op jit(solution)/shard_map/ppermute | solution.py:23
  443.4 38.5 %collective-permute-start.32 = (bf16[384,1024]{1,0:T(8,128)(2,1)}, bf16[384,1024]{1,0:T(8,128)(2,1)}, u32[]{:S(2)}, u32[]{:S(2)}) collective-permute-start(bf16[384,1024]{1,0:T(8,128)(2,1)} %add_convert_fusion.7), channel_id=1, source_target_pairs={{0,24},{4,28},{8,0},{12,4},{16,8},{20,12},{24,16},{28,20},{1,25},{... | collective-permute-start | bytes 2359304 | tf_op jit(solution)/shard_map/ppermute | solution.py:23
  (37 other events, 1345.3 us)
where the time goes:
time: 496 us; the launch traced here: 491 us
  waiting for transfers between devices  284 us (57%)
  starting transfers between devices  89.2 us (18%)
  other arithmetic  44.4 us (9%)
  local copies, waits for them, and re-layouts  39.6 us (8%)
  matrix products  24.2 us (5%)
  blocking collectives  8.42 us (2%)
    ppermute x27, waiting for transfers between devices, send_f(): return lax.ppermute(value, 'fsdp', pairs)  218 us
    ppermute x27, starting transfers between devices, send_f(): return lax.ppermute(value, 'fsdp', pairs)  79.1 us
    ppermute x14, waiting for transfers between devices, send_axis(): lax.ppermute(value, axis, [(i, (i + step) % count) for i in range(count)])  66.5 us
    concatenate x1, other arithmetic, block_update(): full = jnp.concatenate(columns, axis=1)  28.5 us
    dynamic_update_slice x21, local copies, waits for them, and re-layouts, move_weight(): lax.dynamic_update_slice_in_dim(whole, piece, place(owner) * width, join_...  17.5 us
    ppermute x14, starting transfers between devices, send_axis(): lax.ppermute(value, axis, [(i, (i + step) % count) for i in range(count)])  10.1 us
  transfers between devices with their start and end apart: 41, of which 22 were waited for; matrix products, arithmetic and copies ran while one was open for 9% of the time, Pallas kernels for 0%

commit v1 on v0

--- a/solution.py
+++ b/solution.py
@@ -74,9 +74,17 @@
             columns.append(jnp.concatenate(moved, axis=0))
         for step in range(1, count_c):
             columns = columns + [send_axis(piece, "dp", count_c, -step) for piece in columns[:count_t]]
-        full = jnp.concatenate(columns, axis=1)
-        gate_sum = jnp.dot(full, gate_full, preferred_element_type=jnp.float32)
-        up_sum = jnp.dot(full, up_full, preferred_element_type=jnp.float32)
+        gate_sum, up_sum = (
+            sum(
+                jnp.dot(
+                    piece,
+                    weight[k * width : (k + 1) * width],
+                    preferred_element_type=jnp.float32,
+                )
+                for k, piece in enumerate(columns)
+            )
+            for weight in (gate_full, up_full)
+        )
         hidden = (jax.nn.silu(gate_sum) * up_sum).astype(jnp.bfloat16)
         half = count_t * width
         total = None

time: 496 us -> 457 us (0.921)
  waiting for transfers between devices: 284 us -> 200 us
  starting transfers between devices: 89.2 us -> 147 us
  other arithmetic: 44.4 us -> 12.1 us
  matrix products: 24.2 us -> 47.3 us
    ppermute x27, waiting for transfers between devices: 218 us -> 135 us  [send_f(): return lax.ppermute(value, 'fsdp', pairs)]
    ppermute x27, starting transfers between devices: 79.1 us -> 136 us  [send_f(): return lax.ppermute(value, 'fsdp', pairs)]
    concatenate x1 -> x0, other arithmetic: 28.5 us -> none  [block_update(): full = jnp.concatenate(columns, axis=1)]
    dot_general x8, matrix products: 8.02 us -> 20.6 us  [block_update(): jnp.dot(part, down_full[:, k * half:(k + 1) * half], preferred_element_ty...]
    dot_general x2 -> x8, matrix products: 14.3 us -> 26 us  [block_update(): jnp.dot(piece, weight[k * width:(k + 1) * width], preferred_element_type=...]
  transfers between devices with their start and end apart: 41 -> 41, of which waited for: 22 -> 16; matrix products, arithmetic and copies ran while one was open for 9% -> 14% of each run, Pallas kernels for 0% -> 0%
where the time goes in v1:
time: 457 us; the launch traced here: 456 us
  waiting for transfers between devices  200 us (44%)
  starting transfers between devices  147 us (32%)
  matrix products  47.3 us (10%)
  local copies, waits for them, and re-layouts  43.2 us (9%)
  other arithmetic  12.1 us (3%)
  blocking collectives  6.07 us (1%)
    ppermute x27, starting transfers between devices, send_f(): return lax.ppermute(value, 'fsdp', pairs)  136 us
    ppermute x27, waiting for transfers between devices, send_f(): return lax.ppermute(value, 'fsdp', pairs)  135 us
    ppermute x14, waiting for transfers between devices, send_axis(): lax.ppermute(value, axis, [(i, (i + step) % count) for i in range(count)])  64.5 us
    dot_general x8, matrix products, block_update(): jnp.dot(piece, weight[k * width:(k + 1) * width], preferred_element_type=...  26 us
    dot_general x8, matrix products, block_update(): jnp.dot(part, down_full[:, k * half:(k + 1) * half], preferred_element_ty...  20.6 us
    dynamic_update_slice x21, local copies, waits for them, and re-layouts, move_weight(): lax.dynamic_update_slice_in_dim(whole, piece, place(owner) * width, join_...  20.5 us
    ppermute x14, starting transfers between devices, send_axis(): lax.ppermute(value, axis, [(i, (i + step) % count) for i in range(count)])  10.7 us
  transfers between devices with their start and end apart: 41, of which 16 were waited for; matrix products, arithmetic and copies ran while one was open for 14% of the time, Pallas kernels for 0%

profile of v1, /device:TPU:0, one launch (start us, length us, event | category | flops | bytes accessed | tf_op | source)
XLA Modules:
  0.0 455.6 jit_solution(10916176643997849593)
XLA Ops:
  3.1 3.1 collective-permute-start.3
  16.9 4.5 collective-permute-done.3
  21.4 23.4 %collective-permute-start.17 = (bf16[512,512]{1,0:T(8,128)(2,1)}, bf16[512,512]{1,0:T(8,128)(2,1)}, u32[]{:S(2)}, u32[]{:S(2)}) collective-permute-start(bf16[512,512]{1,0:T(8,128)(2,1)} %get-tuple-element.24), channel_id=1, source_target_pairs={{0,16},{4,20},{8,24},{12,28},{16,0},{20,4},{24,8},{28,12},{1,17},{... | collective-permute-start | bytes 1572872 | tf_op jit(solution)/shard_map/ppermute | solution.py:23
  48.9 24.9 %collective-permute-start.18 = (bf16[512,512]{1,0:T(8,128)(2,1)}, bf16[512,512]{1,0:T(8,128)(2,1)}, u32[]{:S(2)}, u32[]{:S(2)}) collective-permute-start(bf16[512,512]{1,0:T(8,128)(2,1)} %get-tuple-element.20), channel_id=1, source_target_pairs={{0,24},{4,28},{8,0},{12,4},{16,8},{20,12},{24,16},{28,20},{1,25},{... | collective-permute-start | bytes 1572872 | tf_op jit(solution)/shard_map/ppermute | solution.py:23
  75.3 9.1 %collective-permute-start.23 = (bf16[512,512]{1,0:T(8,128)(2,1)}, bf16[512,512]{1,0:T(8,128)(2,1)S(1)}, u32[]{:S(2)}, u32[]{:S(2)}) collective-permute-start(bf16[512,512]{1,0:T(8,128)(2,1)} %get-tuple-element.26), channel_id=1, source_target_pairs={{0,8},{4,12},{8,16},{12,20},{16,24},{20,28},{24,0},{28,4},{1,9},{5... | collective-permute-start | bytes 1572872 | tf_op jit(solution)/shard_map/ppermute | solution.py:23
  84.4 5.3 %collective-permute-start.24 = (bf16[512,512]{1,0:T(8,128)(2,1)}, bf16[512,512]{1,0:T(8,128)(2,1)S(1)}, u32[]{:S(2)}, u32[]{:S(2)}) collective-permute-start(bf16[512,512]{1,0:T(8,128)(2,1)} %get-tuple-element.29), channel_id=1, source_target_pairs={{0,16},{4,20},{8,24},{12,28},{16,0},{20,4},{24,8},{28,12},{1,17},{... | collective-permute-start | bytes 1572872 | tf_op jit(solution)/shard_map/ppermute | solution.py:23
  90.5 6.1 %psum.7 = f32[384,1]{0,1:T(1,128)S(1)} all-reduce(f32[384,1]{0,1:T(1,128)S(1)} %broadcast_in_dim.34), channel_id=1, replica_groups=mesh['fsdp'=8,'tensor'=2,'dp'=2] {'tensor','dp'}, use_global_device_ids=true, to_apply=%region_3.4 | all-reduce | flops 384 | bytes 3072 | tf_op jit(solution)/shard_map/psum | solution.py:62
  96.6 13.9 %collective-permute-done.17 = bf16[512,512]{1,0:T(8,128)(2,1)} collective-permute-done((bf16[512,512]{1,0:T(8,128)(2,1)}, bf16[512,512]{1,0:T(8,128)(2,1)}, u32[]{:S(2)}, u32[]{:S(2)}) %collective-permute-start.17) | collective-permute-done | bytes 524320 | tf_op jit(solution)/shard_map/ppermute | solution.py:23
  110.5 2.7 collective-permute-start.25
  113.4 9.8 %collective-permute-start = (bf16[384,1024]{1,0:T(8,128)(2,1)S(1)}, bf16[384,1024]{1,0:T(8,128)(2,1)S(1)}, u32[]{:S(2)}, u32[]{:S(2)}) collective-permute-start(bf16[384,1024]{1,0:T(8,128)(2,1)S(1)} %fusion.8), channel_id=1, source_target_pairs={{0,8},{4,12},{8,16},{12,20},{16,24},{20,28},{24,0},{28,4},{1,9},{5... | collective-permute-start | bytes 2359304 | tf_op jit(solution)/shard_map/ppermute | solution.py:23
  125.5 41.1 %collective-permute-done.24 = bf16[512,512]{1,0:T(8,128)(2,1)S(1)} collective-permute-done((bf16[512,512]{1,0:T(8,128)(2,1)}, bf16[512,512]{1,0:T(8,128)(2,1)S(1)}, u32[]{:S(2)}, u32[]{:S(2)}) %collective-permute-start.24) | collective-permute-done | bytes 524320 | tf_op jit(solution)/shard_map/ppermute | solution.py:23
  186.1 8.6 %collective-permute-done.1 = bf16[384,1024]{1,0:T(8,128)(2,1)S(1)} collective-permute-done((bf16[384,1024]{1,0:T(8,128)(2,1)S(1)}, bf16[384,1024]{1,0:T(8,128)(2,1)S(1)}, u32[]{:S(2)}, u32[]{:S(2)}) %collective-permute-start.1) | collective-permute-done | bytes 786464 | tf_op jit(solution)/shard_map/ppermute | solution.py:23
  206.2 8.9 %collective-permute-done.11 = bf16[384,1024]{1,0:T(8,128)(2,1)S(1)} collective-permute-done((bf16[384,1024]{1,0:T(8,128)(2,1)S(1)}, bf16[384,1024]{1,0:T(8,128)(2,1)S(1)}, u32[]{:S(2)}, u32[]{:S(2)}) %collective-permute-start.11) | collective-permute-done | bytes 786464 | tf_op jit(solution)/shard_map/ppermute | solution.py:26
  216.6 15.3 %collective-permute-done.12 = bf16[384,1024]{1,0:T(8,128)(2,1)S(1)} collective-permute-done((bf16[384,1024]{1,0:T(8,128)(2,1)S(1)}, bf16[384,1024]{1,0:T(8,128)(2,1)S(1)}, u32[]{:S(2)}, u32[]{:S(2)}) %collective-permute-start.12) | collective-permute-done | bytes 786464 | tf_op jit(solution)/shard_map/ppermute | solution.py:26
  233.5 14.3 %collective-permute-done.13 = bf16[384,1024]{1,0:T(8,128)(2,1)S(1)} collective-permute-done((bf16[384,1024]{1,0:T(8,128)(2,1)S(1)}, bf16[384,1024]{1,0:T(8,128)(2,1)S(1)}, u32[]{:S(2)}, u32[]{:S(2)}) %collective-permute-start.13) | collective-permute-done | bytes 786464 | tf_op jit(solution)/shard_map/ppermute | solution.py:26
  252.6 10.2 %collective-permute-done.22 = bf16[512,512]{1,0:T(8,128)(2,1)S(1)} collective-permute-done((bf16[512,512]{1,0:T(8,128)(2,1)}, bf16[512,512]{1,0:T(8,128)(2,1)S(1)}, u32[]{:S(2)}, u32[]{:S(2)}) %collective-permute-start.22) | collective-permute-done | bytes 524320 | tf_op jit(solution)/shard_map/ppermute | solution.py:23
  264.4 9.6 %collective-permute-done.27 = bf16[512,512]{1,0:T(8,128)(2,1)S(1)} collective-permute-done((bf16[512,512]{1,0:T(8,128)(2,1)S(1)}, bf16[512,512]{1,0:T(8,128)(2,1)S(1)}, u32[]{:S(2)}, u32[]{:S(2)}) %collective-permute-start.27) | collective-permute-done | bytes 524320 | tf_op jit(solution)/shard_map/ppermute | solution.py:23
  274.9 10.4 %collective-permute-done.28 = bf16[512,512]{1,0:T(8,128)(2,1)S(1)} collective-permute-done((bf16[512,512]{1,0:T(8,128)(2,1)S(1)}, bf16[512,512]{1,0:T(8,128)(2,1)S(1)}, u32[]{:S(2)}, u32[]{:S(2)}) %collective-permute-start.28) | collective-permute-done | bytes 524320 | tf_op jit(solution)/shard_map/ppermute | solution.py:23
  286.1 8.4 %collective-permute-done.29 = bf16[512,512]{1,0:T(8,128)(2,1)S(1)} collective-permute-done((bf16[512,512]{1,0:T(8,128)(2,1)S(1)}, bf16[512,512]{1,0:T(8,128)(2,1)S(1)}, u32[]{:S(2)}, u32[]{:S(2)}) %collective-permute-start.29) | collective-permute-done | bytes 524320 | tf_op jit(solution)/shard_map/ppermute | solution.py:23
  297.2 3.5 fusion.22
  302.5 3.5 fusion.20
  307.9 3.4 fusion.18
  313.3 8.1 %fusion.5 = bf16[1536,512]{1,0:T(8,128)(2,1)S(1)} fusion(f32[1536,512]{1,0:T(8,128)} %fusion.18, f32[1536,512]{1,0:T(8,128)} %fusion.20, f32[1536,512]{1,0:T(8,128)} %fusion.22, f32[1536,512]{1,0:T(8,128)S(1)} %fusion.4, bf16[4096,512]{1,0:T(8,128)(2,1)S(1)} %constant_dynamic-update-slice_fusion.8, bf16[384,1024]{1,0:T(8,128)(2,1)S(1)} %collective-permute-done.2, ...), kind=kOutput, calls=%fused_computation.14 | convolution fusion | flops 1630273536 | bytes 18350080 | tf_op jit(solution)/shard_map/dot_general | solution.py:79
  350.7 13.9 %collective-permute-done.31 = bf16[384,1024]{1,0:T(8,128)(2,1)S(1)} collective-permute-done((bf16[384,1024]{1,0:T(8,128)(2,1)S(1)}, bf16[384,1024]{1,0:T(8,128)(2,1)S(1)}, u32[]{:S(2)}, u32[]{:S(2)}) %collective-permute-start.31) | collective-permute-done | bytes 786464 | tf_op jit(solution)/shard_map/ppermute | solution.py:26
  364.9 16.6 %collective-permute-start.32 = (bf16[384,1024]{1,0:T(8,128)(2,1)S(1)}, bf16[384,1024]{1,0:T(8,128)(2,1)}, u32[]{:S(2)}, u32[]{:S(2)}) collective-permute-start(bf16[384,1024]{1,0:T(8,128)(2,1)S(1)} %add_convert_fusion.7), channel_id=1, source_target_pairs={{0,24},{4,28},{8,0},{12,4},{16,8},{20,12},{24,16},{28,20},{1,25},{... | collective-permute-start | bytes 2359304 | tf_op jit(solution)/shard_map/ppermute | solution.py:23
  381.8 4.3 collective-permute-start.35
  386.1 12.2 %collective-permute-done.37 = bf16[384,1024]{1,0:T(8,128)(2,1)S(1)} collective-permute-done((bf16[384,1024]{1,0:T(8,128)(2,1)S(1)}, bf16[384,1024]{1,0:T(8,128)(2,1)S(1)}, u32[]{:S(2)}, u32[]{:S(2)}) %collective-permute-start.37) | collective-permute-done | bytes 786464 | tf_op jit(solution)/shard_map/ppermute | solution.py:26
  399.5 13.7 %collective-permute-start.38 = (bf16[384,1024]{1,0:T(8,128)(2,1)}, bf16[384,1024]{1,0:T(8,128)(2,1)}, u32[]{:S(2)}, u32[]{:S(2)}) collective-permute-start(bf16[384,1024]{1,0:T(8,128)(2,1)} %add_convert_fusion.5), channel_id=1, source_target_pairs={{0,8},{4,12},{8,16},{12,20},{16,24},{20,28},{24,0},{28,4},{1,9},{5... | collective-permute-start | bytes 2359304 | tf_op jit(solution)/shard_map/ppermute | solution.py:23
  413.3 8.1 %gather_fusion.1 = bf16[512,1024]{1,0:T(8,128)(2,1)} fusion(bf16[8,64,1024]{2,1,0:T(8,128)(2,1)S(1)} %bitcast.19, s32[512]{0:T(512)S(1)} %reshape.108), kind=kCustom, calls=%fused_computation.1 | custom fusion | bytes 2101248 | tf_op jit(solution)/shard_map/vmap()/gather | solution.py:126
  421.5 25.0 %collective-permute-done.35 = bf16[384,1024]{1,0:T(8,128)(2,1)} collective-permute-done((bf16[384,1024]{1,0:T(8,128)(2,1)S(1)}, bf16[384,1024]{1,0:T(8,128)(2,1)}, u32[]{:S(2)}, u32[]{:S(2)}) %collective-permute-start.35) | collective-permute-done | bytes 786464 | tf_op jit(solution)/shard_map/ppermute | solution.py:23
  446.5 2.8 add_add_fusion
  452.0 3.6 fusion.17
  (160 shorter events, 106.9 us)
Async XLA Ops:
  6.1 42.7 %collective-permute-start.4 = (bf16[512,512]{1,0:T(8,128)(2,1)}, bf16[512,512]{1,0:T(8,128)(2,1)}, u32[]{:S(2)}, u32[]{:S(2)}) collective-permute-start(bf16[512,512]{1,0:T(8,128)(2,1)} %get-tuple-element.19), channel_id=1, source_target_pairs={{0,16},{4,20},{8,24},{12,28},{16,0},{20,4},{24,8},{28,12},{1,17},{... | collective-permute-start | bytes 1572872 | tf_op jit(solution)/shard_map/ppermute | solution.py:23
  8.7 65.0 %collective-permute-start.5 = (bf16[512,512]{1,0:T(8,128)(2,1)}, bf16[512,512]{1,0:T(8,128)(2,1)}, u32[]{:S(2)}, u32[]{:S(2)}) collective-permute-start(bf16[512,512]{1,0:T(8,128)(2,1)} %get-tuple-element.15), channel_id=1, source_target_pairs={{0,24},{4,28},{8,0},{12,4},{16,8},{20,12},{24,16},{28,20},{1,25},{... | collective-permute-start | bytes 1572872 | tf_op jit(solution)/shard_map/ppermute | solution.py:23
  10.1 65.2 %collective-permute-start.6 = (bf16[512,512]{1,0:T(8,128)(2,1)}, bf16[512,512]{1,0:T(8,128)(2,1)}, u32[]{:S(2)}, u32[]{:S(2)}) collective-permute-start(bf16[512,512]{1,0:T(8,128)(2,1)} %get-tuple-element.18), channel_id=1, source_target_pairs={{0,4},{4,0},{8,12},{12,8},{16,20},{20,16},{24,28},{28,24},{1,5},{5... | collective-permute-start | bytes 1572872 | tf_op jit(solution)/shard_map/ppermute | solution.py:23
  15.4 69.0 %collective-permute-start.16 = (bf16[512,512]{1,0:T(8,128)(2,1)}, bf16[512,512]{1,0:T(8,128)(2,1)}, u32[]{:S(2)}, u32[]{:S(2)}) collective-permute-start(bf16[512,512]{1,0:T(8,128)(2,1)} %get-tuple-element.21), channel_id=1, source_target_pairs={{0,8},{4,12},{8,16},{12,20},{16,24},{20,28},{24,0},{28,4},{1,9},{5... | collective-permute-start | bytes 1572872 | tf_op jit(solution)/shard_map/ppermute | solution.py:23
  21.4 89.1 %collective-permute-start.17 = (bf16[512,512]{1,0:T(8,128)(2,1)}, bf16[512,512]{1,0:T(8,128)(2,1)}, u32[]{:S(2)}, u32[]{:S(2)}) collective-permute-start(bf16[512,512]{1,0:T(8,128)(2,1)} %get-tuple-element.24), channel_id=1, source_target_pairs={{0,16},{4,20},{8,24},{12,28},{16,0},{20,4},{24,8},{28,12},{1,17},{... | collective-permute-start | bytes 1572872 | tf_op jit(solution)/shard_map/ppermute | solution.py:23
  48.9 64.5 %collective-permute-start.18 = (bf16[512,512]{1,0:T(8,128)(2,1)}, bf16[512,512]{1,0:T(8,128)(2,1)}, u32[]{:S(2)}, u32[]{:S(2)}) collective-permute-start(bf16[512,512]{1,0:T(8,128)(2,1)} %get-tuple-element.20), channel_id=1, source_target_pairs={{0,24},{4,28},{8,0},{12,4},{16,8},{20,12},{24,16},{28,20},{1,25},{... | collective-permute-start | bytes 1572872 | tf_op jit(solution)/shard_map/ppermute | solution.py:23
  73.8 49.4 %collective-permute-start.19 = (bf16[512,512]{1,0:T(8,128)(2,1)}, bf16[512,512]{1,0:T(8,128)(2,1)}, u32[]{:S(2)}, u32[]{:S(2)}) collective-permute-start(bf16[512,512]{1,0:T(8,128)(2,1)} %get-tuple-element.23), channel_id=1, source_target_pairs={{0,4},{4,0},{8,12},{12,8},{16,20},{20,16},{24,28},{28,24},{1,5},{5... | collective-permute-start | bytes 1572872 | tf_op jit(solution)/shard_map/ppermute | solution.py:23
  75.3 47.9 %collective-permute-start.23 = (bf16[512,512]{1,0:T(8,128)(2,1)}, bf16[512,512]{1,0:T(8,128)(2,1)S(1)}, u32[]{:S(2)}, u32[]{:S(2)}) collective-permute-start(bf16[512,512]{1,0:T(8,128)(2,1)} %get-tuple-element.26), channel_id=1, source_target_pairs={{0,8},{4,12},{8,16},{12,20},{16,24},{20,28},{24,0},{28,4},{1,9},{5... | collective-permute-start | bytes 1572872 | tf_op jit(solution)/shard_map/ppermute | solution.py:23
  84.4 82.2 %collective-permute-start.24 = (bf16[512,512]{1,0:T(8,128)(2,1)}, bf16[512,512]{1,0:T(8,128)(2,1)S(1)}, u32[]{:S(2)}, u32[]{:S(2)}) collective-permute-start(bf16[512,512]{1,0:T(8,128)(2,1)} %get-tuple-element.29), channel_id=1, source_target_pairs={{0,16},{4,20},{8,24},{12,28},{16,0},{20,4},{24,8},{28,12},{1,17},{... | collective-permute-start | bytes 1572872 | tf_op jit(solution)/shard_map/ppermute | solution.py:23
  110.5 63.3 %collective-permute-start.25 = (bf16[512,512]{1,0:T(8,128)(2,1)}, bf16[512,512]{1,0:T(8,128)(2,1)S(1)}, u32[]{:S(2)}, u32[]{:S(2)}) collective-permute-start(bf16[512,512]{1,0:T(8,128)(2,1)} %get-tuple-element.25), channel_id=1, source_target_pairs={{0,24},{4,28},{8,0},{12,4},{16,8},{20,12},{24,16},{28,20},{1,25},{... | collective-permute-start | bytes 1572872 | tf_op jit(solution)/shard_map/ppermute | solution.py:23
  113.4 72.2 %collective-permute-start = (bf16[384,1024]{1,0:T(8,128)(2,1)S(1)}, bf16[384,1024]{1,0:T(8,128)(2,1)S(1)}, u32[]{:S(2)}, u32[]{:S(2)}) collective-permute-start(bf16[384,1024]{1,0:T(8,128)(2,1)S(1)} %fusion.8), channel_id=1, source_target_pairs={{0,8},{4,12},{8,16},{12,20},{16,24},{20,28},{24,0},{28,4},{1,9},{5... | collective-permute-start | bytes 2359304 | tf_op jit(solution)/shard_map/ppermute | solution.py:23
  123.2 71.5 %collective-permute-start.1 = (bf16[384,1024]{1,0:T(8,128)(2,1)S(1)}, bf16[384,1024]{1,0:T(8,128)(2,1)S(1)}, u32[]{:S(2)}, u32[]{:S(2)}) collective-permute-start(bf16[384,1024]{1,0:T(8,128)(2,1)S(1)} %fusion.8), channel_id=1, source_target_pairs={{0,16},{4,20},{8,24},{12,28},{16,0},{20,4},{24,8},{28,12},{1,17},{... | collective-permute-start | bytes 2359304 | tf_op jit(solution)/shard_map/ppermute | solution.py:23
  123.2 73.0 %collective-permute-start.2 = (bf16[384,1024]{1,0:T(8,128)(2,1)S(1)}, bf16[384,1024]{1,0:T(8,128)(2,1)S(1)}, u32[]{:S(2)}, u32[]{:S(2)}) collective-permute-start(bf16[384,1024]{1,0:T(8,128)(2,1)S(1)} %fusion.8), channel_id=1, source_target_pairs={{0,24},{4,28},{8,0},{12,4},{16,8},{20,12},{24,16},{28,20},{1,25},{... | collective-permute-start | bytes 2359304 | tf_op jit(solution)/shard_map/ppermute | solution.py:23
  173.8 23.3 %collective-permute-start.10 = (bf16[384,1024]{1,0:T(8,128)(2,1)S(1)}, bf16[384,1024]{1,0:T(8,128)(2,1)S(1)}, u32[]{:S(2)}, u32[]{:S(2)}) collective-permute-start(bf16[384,1024]{1,0:T(8,128)(2,1)S(1)} %fusion.8), channel_id=1, source_target_pairs={{0,2},{2,0},{1,3},{3,1},{4,6},{6,4},{5,7},{7,5},{8,10},{10,8},{9,1... | collective-permute-start | bytes 2359304 | tf_op jit(solution)/shard_map/ppermute | solution.py:26
  185.6 19.1 %collective-permute-start.8 = (bf16[512,512]{1,0:T(8,128)(2,1)}, bf16[512,512]{1,0:T(8,128)(2,1)S(1)}, u32[]{:S(2)}, u32[]{:S(2)}) collective-permute-start(bf16[512,512]{1,0:T(8,128)(2,1)} %collective-permute-done.4), channel_id=1, source_target_pairs={{0,4},{4,0},{8,12},{12,8},{16,20},{20,16},{24,28},{28,24},{1,5},{5... | collective-permute-start | bytes 1572872 | tf_op jit(solution)/shard_map/ppermute | solution.py:23
  194.7 20.4 %collective-permute-start.11 = (bf16[384,1024]{1,0:T(8,128)(2,1)S(1)}, bf16[384,1024]{1,0:T(8,128)(2,1)S(1)}, u32[]{:S(2)}, u32[]{:S(2)}) collective-permute-start(bf16[384,1024]{1,0:T(8,128)(2,1)S(1)} %collective-permute-done), channel_id=1, source_target_pairs={{0,2},{2,0},{1,3},{3,1},{4,6},{6,4},{5,7},{7,5},{8,10},{10,8},{9,1... | collective-permute-start | bytes 2359304 | tf_op jit(solution)/shard_map/ppermute | solution.py:26
  196.2 35.7 %collective-permute-start.12 = (bf16[384,1024]{1,0:T(8,128)(2,1)S(1)}, bf16[384,1024]{1,0:T(8,128)(2,1)S(1)}, u32[]{:S(2)}, u32[]{:S(2)}) collective-permute-start(bf16[384,1024]{1,0:T(8,128)(2,1)S(1)} %collective-permute-done.1), channel_id=1, source_target_pairs={{0,2},{2,0},{1,3},{3,1},{4,6},{6,4},{5,7},{7,5},{8,10},{10,8},{9,1... | collective-permute-start | bytes 2359304 | tf_op jit(solution)/shard_map/ppermute | solution.py:26
  197.1 103.6 %collective-permute-start.14 = (bf16[1536,1024]{1,0:T(8,128)(2,1)S(1)}, bf16[1536,1024]{1,0:T(8,128)(2,1)S(1)}, u32[]{:S(2)}, u32[]{:S(2)}) collective-permute-start(bf16[1536,1024]{1,0:T(8,128)(2,1)S(1)} %pad_maximum_fusion), channel_id=1, source_target_pairs={{0,1},{1,0},{2,3},{3,2},{4,5},{5,4},{6,7},{7,6},{8,9},{9,8},{10,11... | collective-permute-start | bytes 9437192 | tf_op jit(solution)/shard_map/ppermute | solution.py:26
  197.2 50.6 %collective-permute-start.13 = (bf16[384,1024]{1,0:T(8,128)(2,1)S(1)}, bf16[384,1024]{1,0:T(8,128)(2,1)S(1)}, u32[]{:S(2)}, u32[]{:S(2)}) collective-permute-start(bf16[384,1024]{1,0:T(8,128)(2,1)S(1)} %collective-permute-done.2), channel_id=1, source_target_pairs={{0,2},{2,0},{1,3},{3,1},{4,6},{6,4},{5,7},{7,5},{8,10},{10,8},{9,1... | collective-permute-start | bytes 2359304 | tf_op jit(solution)/shard_map/ppermute | solution.py:26
  204.7 44.6 %collective-permute-start.9 = (bf16[512,512]{1,0:T(8,128)(2,1)}, bf16[512,512]{1,0:T(8,128)(2,1)S(1)}, u32[]{:S(2)}, u32[]{:S(2)}) collective-permute-start(bf16[512,512]{1,0:T(8,128)(2,1)} %collective-permute-done.5), channel_id=1, source_target_pairs={{0,4},{4,0},{8,12},{12,8},{16,20},{20,16},{24,28},{28,24},{1,5},{5... | collective-permute-start | bytes 1572872 | tf_op jit(solution)/shard_map/ppermute | solution.py:23
  215.1 35.2 %collective-permute-start.20 = (bf16[512,512]{1,0:T(8,128)(2,1)}, bf16[512,512]{1,0:T(8,128)(2,1)S(1)}, u32[]{:S(2)}, u32[]{:S(2)}) collective-permute-start(bf16[512,512]{1,0:T(8,128)(2,1)} %collective-permute-done.16), channel_id=1, source_target_pairs={{0,4},{4,0},{8,12},{12,8},{16,20},{20,16},{24,28},{28,24},{1,5},{5... | collective-permute-start | bytes 1572872 | tf_op jit(solution)/shard_map/ppermute | solution.py:23
  249.3 56.8 %collective-permute-start.15 = (bf16[1536,1024]{1,0:T(8,128)(2,1)S(1)}, bf16[1536,1024]{1,0:T(8,128)(2,1)S(1)}, u32[]{:S(2)}, u32[]{:S(2)}) collective-permute-start(bf16[1536,1024]{1,0:T(8,128)(2,1)S(1)} %constant_dynamic-update-slice_fusion.24), channel_id=1, source_target_pairs={{0,1},{1,0},{2,3},{3,2},{4,5},{5,4},{6,7},{7,6},{8,9},{9,8},{10,11... | collective-permute-start | bytes 9437192 | tf_op jit(solution)/shard_map/ppermute | solution.py:26
  250.3 23.7 %collective-permute-start.27 = (bf16[512,512]{1,0:T(8,128)(2,1)S(1)}, bf16[512,512]{1,0:T(8,128)(2,1)S(1)}, u32[]{:S(2)}, u32[]{:S(2)}) collective-permute-start(bf16[512,512]{1,0:T(8,128)(2,1)S(1)} %collective-permute-done.23), channel_id=1, source_target_pairs={{0,4},{4,0},{8,12},{12,8},{16,20},{20,16},{24,28},{28,24},{1,5},{5... | collective-permute-start | bytes 1572872 | tf_op jit(solution)/shard_map/ppermute | solution.py:23
  251.0 34.2 %collective-permute-start.28 = (bf16[512,512]{1,0:T(8,128)(2,1)S(1)}, bf16[512,512]{1,0:T(8,128)(2,1)S(1)}, u32[]{:S(2)}, u32[]{:S(2)}) collective-permute-start(bf16[512,512]{1,0:T(8,128)(2,1)S(1)} %collective-permute-done.24), channel_id=1, source_target_pairs={{0,4},{4,0},{8,12},{12,8},{16,20},{20,16},{24,28},{28,24},{1,5},{5... | collective-permute-start | bytes 1572872 | tf_op jit(solution)/shard_map/ppermute | solution.py:23
  262.8 31.8 %collective-permute-start.29 = (bf16[512,512]{1,0:T(8,128)(2,1)S(1)}, bf16[512,512]{1,0:T(8,128)(2,1)S(1)}, u32[]{:S(2)}, u32[]{:S(2)}) collective-permute-start(bf16[512,512]{1,0:T(8,128)(2,1)S(1)} %collective-permute-done.25), channel_id=1, source_target_pairs={{0,4},{4,0},{8,12},{12,8},{16,20},{20,16},{24,28},{28,24},{1,5},{5... | collective-permute-start | bytes 1572872 | tf_op jit(solution)/shard_map/ppermute | solution.py:23
  344.1 20.5 %collective-permute-start.31 = (bf16[384,1024]{1,0:T(8,128)(2,1)S(1)}, bf16[384,1024]{1,0:T(8,128)(2,1)S(1)}, u32[]{:S(2)}, u32[]{:S(2)}) collective-permute-start(bf16[384,1024]{1,0:T(8,128)(2,1)S(1)} %slice.119), channel_id=1, source_target_pairs={{0,2},{2,0},{1,3},{3,1},{4,6},{6,4},{5,7},{7,5},{8,10},{10,8},{9,1... | collective-permute-start | bytes 2359304 | tf_op jit(solution)/shard_map/ppermute | solution.py:26
  346.4 35.0 %collective-permute-start.34 = (bf16[384,1024]{1,0:T(8,128)(2,1)S(1)}, bf16[384,1024]{1,0:T(8,128)(2,1)S(1)}, u32[]{:S(2)}, u32[]{:S(2)}) collective-permute-start(bf16[384,1024]{1,0:T(8,128)(2,1)S(1)} %slice.122), channel_id=1, source_target_pairs={{0,2},{2,0},{1,3},{3,1},{4,6},{6,4},{5,7},{7,5},{8,10},{10,8},{9,1... | collective-permute-start | bytes 2359304 | tf_op jit(solution)/shard_map/ppermute | solution.py:26
  347.7 50.5 %collective-permute-start.37 = (bf16[384,1024]{1,0:T(8,128)(2,1)S(1)}, bf16[384,1024]{1,0:T(8,128)(2,1)S(1)}, u32[]{:S(2)}, u32[]{:S(2)}) collective-permute-start(bf16[384,1024]{1,0:T(8,128)(2,1)S(1)} %slice.125), channel_id=1, source_target_pairs={{0,2},{2,0},{1,3},{3,1},{4,6},{6,4},{5,7},{7,5},{8,10},{10,8},{9,1... | collective-permute-start | bytes 2359304 | tf_op jit(solution)/shard_map/ppermute | solution.py:26
  350.1 71.4 %collective-permute-start.40 = (bf16[384,1024]{1,0:T(8,128)(2,1)S(1)}, bf16[384,1024]{1,0:T(8,128)(2,1)}, u32[]{:S(2)}, u32[]{:S(2)}) collective-permute-start(bf16[384,1024]{1,0:T(8,128)(2,1)S(1)} %slice.128), channel_id=1, source_target_pairs={{0,2},{2,0},{1,3},{3,1},{4,6},{6,4},{5,7},{7,5},{8,10},{10,8},{9,1... | collective-permute-start | bytes 2359304 | tf_op jit(solution)/shard_map/ppermute | solution.py:26
  364.9 56.7 %collective-permute-start.32 = (bf16[384,1024]{1,0:T(8,128)(2,1)S(1)}, bf16[384,1024]{1,0:T(8,128)(2,1)}, u32[]{:S(2)}, u32[]{:S(2)}) collective-permute-start(bf16[384,1024]{1,0:T(8,128)(2,1)S(1)} %add_convert_fusion.7), channel_id=1, source_target_pairs={{0,24},{4,28},{8,0},{12,4},{16,8},{20,12},{24,16},{28,20},{1,25},{... | collective-permute-start | bytes 2359304 | tf_op jit(solution)/shard_map/ppermute | solution.py:23
  381.8 64.8 %collective-permute-start.35 = (bf16[384,1024]{1,0:T(8,128)(2,1)S(1)}, bf16[384,1024]{1,0:T(8,128)(2,1)}, u32[]{:S(2)}, u32[]{:S(2)}) collective-permute-start(bf16[384,1024]{1,0:T(8,128)(2,1)S(1)} %add_convert_fusion.6), channel_id=1, source_target_pairs={{0,16},{4,20},{8,24},{12,28},{16,0},{20,4},{24,8},{28,12},{1,17},{... | collective-permute-start | bytes 2359304 | tf_op jit(solution)/shard_map/ppermute | solution.py:23
  399.5 47.0 %collective-permute-start.38 = (bf16[384,1024]{1,0:T(8,128)(2,1)}, bf16[384,1024]{1,0:T(8,128)(2,1)}, u32[]{:S(2)}, u32[]{:S(2)}) collective-permute-start(bf16[384,1024]{1,0:T(8,128)(2,1)} %add_convert_fusion.5), channel_id=1, source_target_pairs={{0,8},{4,12},{8,16},{12,20},{16,24},{20,28},{24,0},{28,4},{1,9},{5... | collective-permute-start | bytes 2359304 | tf_op jit(solution)/shard_map/ppermute | solution.py:23
  (23 other events, 982.0 us)

commit v2 on v1

--- a/solution.py
+++ b/solution.py
@@ -20,6 +20,10 @@
         for a in range(ring):
             for b in range(span):
                 pairs.append((a * span + b, ((a + step_a) % ring) * span + (b + step_b) % span))
+        return lax.ppermute(value, "fsdp", pairs)
+
+    def send_line(value, senders, step):
+        pairs = [(a * span + b, (a + step) * span + b) for a in senders for b in range(span)]
         return lax.ppermute(value, "fsdp", pairs)
 
     def send_axis(value, axis, count, step):
@@ -67,7 +71,14 @@
         gate_full = move_weight(gate_weight, 1)
         up_full = move_weight(up_weight, 1)
         down_full = move_weight(down_weight, 0)
-        slots = [normed] + [send_f(normed, k, 0) for k in range(1, ring)]
+        a = lax.axis_index("fsdp") // span
+        rightward, leftward = [normed], [normed]
+        for k in range(1, ring):
+            rightward.append(send_line(rightward[-1], range(k - 1, ring - 1), 1))
+            leftward.append(send_line(leftward[-1], range(1, ring - k + 1), -1))
+        slots = [normed] + [
+            jnp.where(a >= k, rightward[k], leftward[ring - k]) for k in range(1, ring)
+        ]
         columns = [jnp.concatenate(slots, axis=0)]
         for step in range(1, count_t):
             moved = [send_axis(piece, "tensor", count_t, -step) for piece in slots]
@@ -87,8 +98,8 @@
         )
         hidden = (jax.nn.silu(gate_sum) * up_sum).astype(jnp.bfloat16)
         half = count_t * width
-        total = None
-        for slot in list(range(1, ring)) + [0]:
+        sums = {}
+        for slot in sorted(range(1, ring), key=lambda k: -abs(2 * k - ring)) + [0]:
             part = lax.slice_in_dim(hidden, slot * capacity, (slot + 1) * capacity, axis=0)
             products = [
                 jnp.dot(
@@ -105,9 +116,18 @@
                 away = own[:, step * width : (step + 1) * width]
                 moved = send_axis(away, "tensor", count_t, step)
                 mine = mine + moved.astype(jnp.float32)
-            if slot:
-                mine = send_f(mine.astype(jnp.bfloat16), -slot, 0).astype(jnp.float32)
-            total = mine if total is None else total + mine
+            sums[slot] = mine
+        total = sums[0]
+        right = left = None
+        for k in range(ring - 1, 0, -1):
+            own_right, own_left = sums[ring - k], sums[k]
+            if right is not None:
+                own_right, own_left = own_right + right, own_left + left
+            right = send_line(own_right.astype(jnp.bfloat16), range(ring - k), 1)
+            left = send_line(own_left.astype(jnp.bfloat16), range(k, ring), -1)
+            right, left = right.astype(jnp.float32), left.astype(jnp.float32)
+        if right is not None:
+            total = total + right + left
         return total
 
     def body(states, fresh_rows, norm_gain, gate_weight, up_weight, down_weight, halted, refill_index):

time: 457 us -> 469 us (1.026)
  starting transfers between devices: 147 us -> 132 us
  waiting for transfers between devices: 200 us -> 210 us
  matrix products: 47.3 us -> 53.4 us
  other arithmetic: 12.1 us -> 16.8 us
    ppermute x0 -> x12, waiting for transfers between devices: none -> 66.9 us  [send_line(): return lax.ppermute(value, 'fsdp', pairs)]
    ppermute x27 -> x21, starting transfers between devices: 136 us -> 79.3 us  [send_f(): return lax.ppermute(value, 'fsdp', pairs)]
    ppermute x0 -> x12, starting transfers between devices: none -> 41 us  [send_line(): return lax.ppermute(value, 'fsdp', pairs)]
    ppermute x27 -> x21, waiting for transfers between devices: 135 us -> 96 us  [send_f(): return lax.ppermute(value, 'fsdp', pairs)]
    ppermute x14, waiting for transfers between devices: 64.5 us -> 46.6 us  [send_axis(): lax.ppermute(value, axis, [(i, (i + step) % count) for i in range(count)])]
    dot_general x8, matrix products: 26 us -> 30.9 us  [block_update(): jnp.dot(piece, weight[k * width:(k + 1) * width], preferred_element_type=...]
  transfers between devices with their start and end apart: 41 -> 47, of which waited for: 16 -> 20; matrix products, arithmetic and copies ran while one was open for 14% -> 15% of each run, Pallas kernels for 0% -> 0%
where the time goes in v2:
time: 469 us; the launch traced here: 463 us
  waiting for transfers between devices  210 us (45%)
  starting transfers between devices  132 us (28%)
  matrix products  53.4 us (11%)
  local copies, waits for them, and re-layouts  42.4 us (9%)
  other arithmetic  16.8 us (4%)
  blocking collectives  8.4 us (2%)
    ppermute x21, waiting for transfers between devices, send_f(): return lax.ppermute(value, 'fsdp', pairs)  96 us
    ppermute x21, starting transfers between devices, send_f(): return lax.ppermute(value, 'fsdp', pairs)  79.3 us
    ppermute x12, waiting for transfers between devices, send_line(): return lax.ppermute(value, 'fsdp', pairs)  66.9 us
    ppermute x14, waiting for transfers between devices, send_axis(): lax.ppermute(value, axis, [(i, (i + step) % count) for i in range(count)])  46.6 us
    ppermute x12, starting transfers between devices, send_line(): return lax.ppermute(value, 'fsdp', pairs)  41 us
    dot_general x8, matrix products, block_update(): jnp.dot(piece, weight[k * width:(k + 1) * width], preferred_element_type=...  30.9 us
    dot_general x8, matrix products, block_update(): jnp.dot(part, down_full[:, k * half:(k + 1) * half], preferred_element_ty...  20.6 us
    dynamic_update_slice x21, local copies, waits for them, and re-layouts, move_weight(): lax.dynamic_update_slice_in_dim(whole, piece, place(owner) * width, join_...  17.5 us
  transfers between devices with their start and end apart: 47, of which 20 were waited for; matrix products, arithmetic and copies ran while one was open for 15% of the time, Pallas kernels for 0%

profile of v2, /device:TPU:0, one launch (start us, length us, event | category | flops | bytes accessed | tf_op | source)
XLA Modules:
  0.0 463.3 jit_solution(314757496683501208)
XLA Ops:
  3.5 8.4 %psum.7 = f32[384,1]{0,1:T(1,128)S(1)} all-reduce(f32[384,1]{0,1:T(1,128)S(1)} %broadcast_in_dim.34), channel_id=1, replica_groups=mesh['fsdp'=8,'tensor'=2,'dp'=2] {'tensor','dp'}, use_global_device_ids=true, to_apply=%region_3.4 | all-reduce | flops 384 | bytes 3072 | tf_op jit(solution)/shard_map/psum | solution.py:66
  14.1 4.6 collective-permute-start
  24.4 11.5 %collective-permute-done.1 = bf16[384,1024]{1,0:T(8,128)(2,1)S(1)} collective-permute-done((bf16[384,1024]{1,0:T(8,128)(2,1)S(1)}, bf16[384,1024]{1,0:T(8,128)(2,1)S(1)}, u32[]{:S(2)}, u32[]{:S(2)}) %collective-permute-start.1) | collective-permute-done | bytes 786464 | tf_op jit(solution)/shard_map/ppermute | solution.py:27
  40.9 40.8 %collective-permute-start.19 = (bf16[512,512]{1,0:T(8,128)(2,1)}, bf16[512,512]{1,0:T(8,128)(2,1)}, u32[]{:S(2)}, u32[]{:S(2)}) collective-permute-start(bf16[512,512]{1,0:T(8,128)(2,1)} %get-tuple-element.23), channel_id=1, source_target_pairs={{0,8},{4,12},{8,16},{12,20},{16,24},{20,28},{24,0},{28,4},{1,9},{5... | collective-permute-start | bytes 1572872 | tf_op jit(solution)/shard_map/ppermute | solution.py:23
  94.3 7.9 %collective-permute-start.21 = (bf16[512,512]{1,0:T(8,128)(2,1)}, bf16[512,512]{1,0:T(8,128)(2,1)S(1)}, u32[]{:S(2)}, u32[]{:S(2)}) collective-permute-start(bf16[512,512]{1,0:T(8,128)(2,1)} %get-tuple-element.22), channel_id=1, source_target_pairs={{0,24},{4,28},{8,0},{12,4},{16,8},{20,12},{24,16},{28,20},{1,25},{... | collective-permute-start | bytes 1572872 | tf_op jit(solution)/shard_map/ppermute | solution.py:23
  104.1 16.5 %collective-permute-done.20 = bf16[512,512]{1,0:T(8,128)(2,1)} collective-permute-done((bf16[512,512]{1,0:T(8,128)(2,1)}, bf16[512,512]{1,0:T(8,128)(2,1)}, u32[]{:S(2)}, u32[]{:S(2)}) %collective-permute-start.20) | collective-permute-done | bytes 524320 | tf_op jit(solution)/shard_map/ppermute | solution.py:23
  131.6 11.4 %collective-permute-done.21 = bf16[512,512]{1,0:T(8,128)(2,1)S(1)} collective-permute-done((bf16[512,512]{1,0:T(8,128)(2,1)}, bf16[512,512]{1,0:T(8,128)(2,1)S(1)}, u32[]{:S(2)}, u32[]{:S(2)}) %collective-permute-start.21) | collective-permute-done | bytes 524320 | tf_op jit(solution)/shard_map/ppermute | solution.py:23
  143.0 3.7 collective-permute-start.26
  154.3 4.8 %collective-permute-done.26 = bf16[512,512]{1,0:T(8,128)(2,1)S(1)} collective-permute-done((bf16[512,512]{1,0:T(8,128)(2,1)S(1)}, bf16[512,512]{1,0:T(8,128)(2,1)S(1)}, u32[]{:S(2)}, u32[]{:S(2)}) %collective-permute-start.26) | collective-permute-done | bytes 524320 | tf_op jit(solution)/shard_map/ppermute | solution.py:23
  159.1 5.0 %collective-permute-start.28 = (bf16[512,512]{1,0:T(8,128)(2,1)S(1)}, bf16[512,512]{1,0:T(8,128)(2,1)S(1)}, u32[]{:S(2)}, u32[]{:S(2)}) collective-permute-start(bf16[512,512]{1,0:T(8,128)(2,1)S(1)} %copy-done.12), channel_id=1, source_target_pairs={{0,24},{4,28},{8,0},{12,4},{16,8},{20,12},{24,16},{28,20},{1,25},{... | collective-permute-start | bytes 1572872 | tf_op jit(solution)/shard_map/ppermute | solution.py:23
  166.4 10.6 %collective-permute-done.27 = bf16[512,512]{1,0:T(8,128)(2,1)S(1)} collective-permute-done((bf16[512,512]{1,0:T(8,128)(2,1)S(1)}, bf16[512,512]{1,0:T(8,128)(2,1)S(1)}, u32[]{:S(2)}, u32[]{:S(2)}) %collective-permute-start.27) | collective-permute-done | bytes 524320 | tf_op jit(solution)/shard_map/ppermute | solution.py:23
  178.4 10.3 %collective-permute-done.28 = bf16[512,512]{1,0:T(8,128)(2,1)S(1)} collective-permute-done((bf16[512,512]{1,0:T(8,128)(2,1)S(1)}, bf16[512,512]{1,0:T(8,128)(2,1)S(1)}, u32[]{:S(2)}, u32[]{:S(2)}) %collective-permute-start.28) | collective-permute-done | bytes 524320 | tf_op jit(solution)/shard_map/ppermute | solution.py:23
  197.4 25.4 %collective-permute-done.14 = bf16[384,1024]{1,0:T(8,128)(2,1)S(1)} collective-permute-done((bf16[384,1024]{1,0:T(8,128)(2,1)S(1)}, bf16[384,1024]{1,0:T(8,128)(2,1)S(1)}, u32[]{:S(2)}, u32[]{:S(2)}) %collective-permute-start.14) | collective-permute-done | bytes 786464 | tf_op jit(solution)/shard_map/ppermute | solution.py:30
  225.0 6.2 %collective-permute-done.16 = bf16[384,1024]{1,0:T(8,128)(2,1)S(1)} collective-permute-done((bf16[384,1024]{1,0:T(8,128)(2,1)S(1)}, bf16[384,1024]{1,0:T(8,128)(2,1)S(1)}, u32[]{:S(2)}, u32[]{:S(2)}) %collective-permute-start.16) | collective-permute-done | bytes 786464 | tf_op jit(solution)/shard_map/ppermute | solution.py:30
  234.4 7.5 %collective-permute-done.24 = bf16[512,512]{1,0:T(8,128)(2,1)S(1)} collective-permute-done((bf16[512,512]{1,0:T(8,128)(2,1)}, bf16[512,512]{1,0:T(8,128)(2,1)S(1)}, u32[]{:S(2)}, u32[]{:S(2)}) %collective-permute-start.24) | collective-permute-done | bytes 524320 | tf_op jit(solution)/shard_map/ppermute | solution.py:23
  242.6 10.7 %collective-permute-done.25 = bf16[512,512]{1,0:T(8,128)(2,1)S(1)} collective-permute-done((bf16[512,512]{1,0:T(8,128)(2,1)S(1)}, bf16[512,512]{1,0:T(8,128)(2,1)S(1)}, u32[]{:S(2)}, u32[]{:S(2)}) %collective-permute-start.25) | collective-permute-done | bytes 524320 | tf_op jit(solution)/shard_map/ppermute | solution.py:23
  253.9 10.6 %collective-permute-done.30 = bf16[512,512]{1,0:T(8,128)(2,1)S(1)} collective-permute-done((bf16[512,512]{1,0:T(8,128)(2,1)S(1)}, bf16[512,512]{1,0:T(8,128)(2,1)S(1)}, u32[]{:S(2)}, u32[]{:S(2)}) %collective-permute-start.30) | collective-permute-done | bytes 524320 | tf_op jit(solution)/shard_map/ppermute | solution.py:23
  265.3 7.5 %collective-permute-done.31 = bf16[512,512]{1,0:T(8,128)(2,1)S(1)} collective-permute-done((bf16[512,512]{1,0:T(8,128)(2,1)S(1)}, bf16[512,512]{1,0:T(8,128)(2,1)S(1)}, u32[]{:S(2)}, u32[]{:S(2)}) %collective-permute-start.31) | collective-permute-done | bytes 524320 | tf_op jit(solution)/shard_map/ppermute | solution.py:23
  273.7 4.8 %collective-permute-done.32 = bf16[512,512]{1,0:T(8,128)(2,1)S(1)} collective-permute-done((bf16[512,512]{1,0:T(8,128)(2,1)S(1)}, bf16[512,512]{1,0:T(8,128)(2,1)S(1)}, u32[]{:S(2)}, u32[]{:S(2)}) %collective-permute-start.32) | collective-permute-done | bytes 524320 | tf_op jit(solution)/shard_map/ppermute | solution.py:23
  281.1 3.5 fusion.24
  293.3 6.6 %fusion.4 = f32[1536,512]{1,0:T(8,128)S(1)} fusion(f32[1536,512]{1,0:T(8,128)} %fusion.27, f32[1536,512]{1,0:T(8,128)S(1)} %fusion.29, f32[1536,512]{1,0:T(8,128)S(1)} %fusion.31, bf16[4096,512]{1,0:T(8,128)(2,1)S(1)} %constant_dynamic-update-slice_fusion.16, bf16[384,1024]{1,0:T(8,128)(2,1)S(1)} %broadcast_select_fusion, ...), kind=kOutput, calls=%fused_computation.8 | convolution fusion | flops 1625554944 | bytes 16777216 | tf_op jit(solution)/shard_map/dot_general | solution.py:90
  303.3 6.9 %fusion.5 = bf16[1536,512]{1,0:T(8,128)(2,1)S(1)} fusion(f32[1536,512]{1,0:T(8,128)} %fusion.20, f32[1536,512]{1,0:T(8,128)S(1)} %copy-done.19, f32[1536,512]{1,0:T(8,128)S(1)} %copy-done.18, f32[1536,512]{1,0:T(8,128)S(1)} %fusion.4, bf16[4096,512]{1,0:T(8,128)(2,1)S(1)} %constant_dynamic-update-slice_fusion.8, ...), kind=kOutput, calls=%fused_computation.14 | convolution fusion | flops 1630273536 | bytes 18350080 | tf_op jit(solution)/shard_map/dot_general | solution.py:90
  327.6 15.0 %collective-permute-done.40 = bf16[384,1024]{1,0:T(8,128)(2,1)S(1)} collective-permute-done((bf16[384,1024]{1,0:T(8,128)(2,1)S(1)}, bf16[384,1024]{1,0:T(8,128)(2,1)S(1)}, u32[]{:S(2)}, u32[]{:S(2)}) %collective-permute-start.40) | collective-permute-done | bytes 786464 | tf_op jit(solution)/shard_map/ppermute | solution.py:30
  342.9 18.0 %collective-permute-start.41 = (bf16[384,1024]{1,0:T(8,128)(2,1)S(1)}, bf16[384,1024]{1,0:T(8,128)(2,1)S(1)}, u32[]{:S(2)}, u32[]{:S(2)}) collective-permute-start(bf16[384,1024]{1,0:T(8,128)(2,1)S(1)} %fusion.10), channel_id=1, source_target_pairs={{0,8},{4,12},{1,9},{5,13},{2,10},{6,14},{3,11},{7,15}} | collective-permute-start | bytes 2359304 | tf_op jit(solution)/shard_map/ppermute | solution.py:27
  365.8 10.9 %collective-permute-done.41 = bf16[384,1024]{1,0:T(8,128)(2,1)S(1)} collective-permute-done((bf16[384,1024]{1,0:T(8,128)(2,1)S(1)}, bf16[384,1024]{1,0:T(8,128)(2,1)S(1)}, u32[]{:S(2)}, u32[]{:S(2)}) %collective-permute-start.41) | collective-permute-done | bytes 786464 | tf_op jit(solution)/shard_map/ppermute | solution.py:27
  377.2 4.4 collective-permute-start.42
  384.3 12.5 %collective-permute-done.42 = bf16[384,1024]{1,0:T(8,128)(2,1)S(1)} collective-permute-done((bf16[384,1024]{1,0:T(8,128)(2,1)S(1)}, bf16[384,1024]{1,0:T(8,128)(2,1)S(1)}, u32[]{:S(2)}, u32[]{:S(2)}) %collective-permute-start.42) | collective-permute-done | bytes 786464 | tf_op jit(solution)/shard_map/ppermute | solution.py:27
  406.0 5.0 %collective-permute-start.43 = (bf16[384,1024]{1,0:T(8,128)(2,1)}, bf16[384,1024]{1,0:T(8,128)(2,1)S(1)}, u32[]{:S(2)}, u32[]{:S(2)}) collective-permute-start(bf16[384,1024]{1,0:T(8,128)(2,1)} %get-tuple-element.15), channel_id=1, source_target_pairs={{0,8},{4,12},{8,16},{12,20},{16,24},{20,28},{1,9},{5,13},{9,17},{1... | collective-permute-start | bytes 2359304 | tf_op jit(solution)/shard_map/ppermute | solution.py:27
  413.8 7.9 %gather_fusion.1 = bf16[512,1024]{1,0:T(8,128)(2,1)} fusion(bf16[8,64,1024]{2,1,0:T(8,128)(2,1)S(1)} %bitcast.19, s32[512]{0:T(512)S(1)} %reshape.108), kind=kCustom, calls=%fused_computation.1 | custom fusion | bytes 2101248 | tf_op jit(solution)/shard_map/vmap()/gather | solution.py:146
  421.8 3.6 collective-permute-done.43
  426.3 28.3 %collective-permute-done.46 = bf16[384,1024]{1,0:T(8,128)(2,1)} collective-permute-done((bf16[384,1024]{1,0:T(8,128)(2,1)}, bf16[384,1024]{1,0:T(8,128)(2,1)}, u32[]{:S(2)}, u32[]{:S(2)}) %collective-permute-start.46) | collective-permute-done | bytes 786464 | tf_op jit(solution)/shard_map/ppermute | solution.py:27
  459.4 3.6 fusion.19
  (189 shorter events, 127.6 us)
Async XLA Ops:
  12.8 23.1 %collective-permute-start.1 = (bf16[384,1024]{1,0:T(8,128)(2,1)S(1)}, bf16[384,1024]{1,0:T(8,128)(2,1)S(1)}, u32[]{:S(2)}, u32[]{:S(2)}) collective-permute-start(bf16[384,1024]{1,0:T(8,128)(2,1)S(1)} %fusion.8), channel_id=1, source_target_pairs={{8,0},{12,4},{16,8},{20,12},{24,16},{28,20},{9,1},{13,5},{17,9},{2... | collective-permute-start | bytes 2359304 | tf_op jit(solution)/shard_map/ppermute | solution.py:27
  14.1 70.7 %collective-permute-start = (bf16[384,1024]{1,0:T(8,128)(2,1)S(1)}, bf16[384,1024]{1,0:T(8,128)(2,1)S(1)}, u32[]{:S(2)}, u32[]{:S(2)}) collective-permute-start(bf16[384,1024]{1,0:T(8,128)(2,1)S(1)} %fusion.8), channel_id=1, source_target_pairs={{0,8},{4,12},{8,16},{12,20},{16,24},{20,28},{1,9},{5,13},{9,17},{1... | collective-permute-start | bytes 2359304 | tf_op jit(solution)/shard_map/ppermute | solution.py:27
  21.7 59.9 %collective-permute-start.6 = (bf16[512,512]{1,0:T(8,128)(2,1)S(1)}, bf16[512,512]{1,0:T(8,128)(2,1)S(1)}, u32[]{:S(2)}, u32[]{:S(2)}) collective-permute-start(bf16[512,512]{1,0:T(8,128)(2,1)S(1)} %get-tuple-element.18), channel_id=1, source_target_pairs={{0,8},{4,12},{8,16},{12,20},{16,24},{20,28},{24,0},{28,4},{1,9},{5... | collective-permute-start | bytes 1572872 | tf_op jit(solution)/shard_map/ppermute | solution.py:23
  23.3 67.4 %collective-permute-start.7 = (bf16[512,512]{1,0:T(8,128)(2,1)}, bf16[512,512]{1,0:T(8,128)(2,1)}, u32[]{:S(2)}, u32[]{:S(2)}) collective-permute-start(bf16[512,512]{1,0:T(8,128)(2,1)} %get-tuple-element.21), channel_id=1, source_target_pairs={{0,16},{4,20},{8,24},{12,28},{16,0},{20,4},{24,8},{28,12},{1,17},{... | collective-permute-start | bytes 1572872 | tf_op jit(solution)/shard_map/ppermute | solution.py:23
  35.9 88.1 %collective-permute-start.2 = (bf16[384,1024]{1,0:T(8,128)(2,1)S(1)}, bf16[384,1024]{1,0:T(8,128)(2,1)}, u32[]{:S(2)}, u32[]{:S(2)}) collective-permute-start(bf16[384,1024]{1,0:T(8,128)(2,1)S(1)} %collective-permute-done.1), channel_id=1, source_target_pairs={{8,0},{12,4},{16,8},{20,12},{9,1},{13,5},{17,9},{21,13},{10,2},{14... | collective-permute-start | bytes 2359304 | tf_op jit(solution)/shard_map/ppermute | solution.py:27
  40.9 53.4 %collective-permute-start.19 = (bf16[512,512]{1,0:T(8,128)(2,1)}, bf16[512,512]{1,0:T(8,128)(2,1)}, u32[]{:S(2)}, u32[]{:S(2)}) collective-permute-start(bf16[512,512]{1,0:T(8,128)(2,1)} %get-tuple-element.23), channel_id=1, source_target_pairs={{0,8},{4,12},{8,16},{12,20},{16,24},{20,28},{24,0},{28,4},{1,9},{5... | collective-permute-start | bytes 1572872 | tf_op jit(solution)/shard_map/ppermute | solution.py:23
  82.5 38.1 %collective-permute-start.20 = (bf16[512,512]{1,0:T(8,128)(2,1)}, bf16[512,512]{1,0:T(8,128)(2,1)}, u32[]{:S(2)}, u32[]{:S(2)}) collective-permute-start(bf16[512,512]{1,0:T(8,128)(2,1)} %get-tuple-element.26), channel_id=1, source_target_pairs={{0,16},{4,20},{8,24},{12,28},{16,0},{20,4},{24,8},{28,12},{1,17},{... | collective-permute-start | bytes 1572872 | tf_op jit(solution)/shard_map/ppermute | solution.py:23
  84.8 62.0 %collective-permute-start.4 = (bf16[384,1024]{1,0:T(8,128)(2,1)S(1)}, bf16[384,1024]{1,0:T(8,128)(2,1)}, u32[]{:S(2)}, u32[]{:S(2)}) collective-permute-start(bf16[384,1024]{1,0:T(8,128)(2,1)S(1)} %collective-permute-done), channel_id=1, source_target_pairs={{8,16},{12,20},{16,24},{20,28},{9,17},{13,21},{17,25},{21,29},{10,... | collective-permute-start | bytes 2359304 | tf_op jit(solution)/shard_map/ppermute | solution.py:27
  90.6 38.6 %collective-permute-start.8 = (bf16[512,512]{1,0:T(8,128)(2,1)}, bf16[512,512]{1,0:T(8,128)(2,1)}, u32[]{:S(2)}, u32[]{:S(2)}) collective-permute-start(bf16[512,512]{1,0:T(8,128)(2,1)} %get-tuple-element.17), channel_id=1, source_target_pairs={{0,24},{4,28},{8,0},{12,4},{16,8},{20,12},{24,16},{28,20},{1,25},{... | collective-permute-start | bytes 1572872 | tf_op jit(solution)/shard_map/ppermute | solution.py:23
  94.3 48.7 %collective-permute-start.21 = (bf16[512,512]{1,0:T(8,128)(2,1)}, bf16[512,512]{1,0:T(8,128)(2,1)S(1)}, u32[]{:S(2)}, u32[]{:S(2)}) collective-permute-start(bf16[512,512]{1,0:T(8,128)(2,1)} %get-tuple-element.22), channel_id=1, source_target_pairs={{0,24},{4,28},{8,0},{12,4},{16,8},{20,12},{24,16},{28,20},{1,25},{... | collective-permute-start | bytes 1572872 | tf_op jit(solution)/shard_map/ppermute | solution.py:23
  120.6 27.7 %collective-permute-start.9 = (bf16[512,512]{1,0:T(8,128)(2,1)}, bf16[512,512]{1,0:T(8,128)(2,1)S(1)}, u32[]{:S(2)}, u32[]{:S(2)}) collective-permute-start(bf16[512,512]{1,0:T(8,128)(2,1)} %get-tuple-element.20), channel_id=1, source_target_pairs={{0,4},{4,0},{8,12},{12,8},{16,20},{20,16},{24,28},{28,24},{1,5},{5... | collective-permute-start | bytes 1572872 | tf_op jit(solution)/shard_map/ppermute | solution.py:23
  124.0 40.1 %collective-permute-start.3 = (bf16[384,1024]{1,0:T(8,128)(2,1)}, bf16[384,1024]{1,0:T(8,128)(2,1)S(1)}, u32[]{:S(2)}, u32[]{:S(2)}) collective-permute-start(bf16[384,1024]{1,0:T(8,128)(2,1)} %collective-permute-done.2), channel_id=1, source_target_pairs={{8,0},{12,4},{9,1},{13,5},{10,2},{14,6},{11,3},{15,7}} | collective-permute-start | bytes 2359304 | tf_op jit(solution)/shard_map/ppermute | solution.py:27
  129.2 22.8 %collective-permute-start.22 = (bf16[512,512]{1,0:T(8,128)(2,1)S(1)}, bf16[512,512]{1,0:T(8,128)(2,1)S(1)}, u32[]{:S(2)}, u32[]{:S(2)}) collective-permute-start(bf16[512,512]{1,0:T(8,128)(2,1)S(1)} %copy-done.10), channel_id=1, source_target_pairs={{0,4},{4,0},{8,12},{12,8},{16,20},{20,16},{24,28},{28,24},{1,5},{5... | collective-permute-start | bytes 1572872 | tf_op jit(solution)/shard_map/ppermute | solution.py:23
  148.3 43.3 %collective-permute-start.13 = (bf16[384,1024]{1,0:T(8,128)(2,1)S(1)}, bf16[384,1024]{1,0:T(8,128)(2,1)S(1)}, u32[]{:S(2)}, u32[]{:S(2)}) collective-permute-start(bf16[384,1024]{1,0:T(8,128)(2,1)S(1)} %fusion.8), channel_id=1, source_target_pairs={{0,2},{2,0},{1,3},{3,1},{4,6},{6,4},{5,7},{7,5},{8,10},{10,8},{9,1... | collective-permute-start | bytes 2359304 | tf_op jit(solution)/shard_map/ppermute | solution.py:30
  152.0 24.9 %collective-permute-start.27 = (bf16[512,512]{1,0:T(8,128)(2,1)S(1)}, bf16[512,512]{1,0:T(8,128)(2,1)S(1)}, u32[]{:S(2)}, u32[]{:S(2)}) collective-permute-start(bf16[512,512]{1,0:T(8,128)(2,1)S(1)} %copy-done.13), channel_id=1, source_target_pairs={{0,16},{4,20},{8,24},{12,28},{16,0},{20,4},{24,8},{28,12},{1,17},{... | collective-permute-start | bytes 1572872 | tf_op jit(solution)/shard_map/ppermute | solution.py:23
  159.1 29.7 %collective-permute-start.28 = (bf16[512,512]{1,0:T(8,128)(2,1)S(1)}, bf16[512,512]{1,0:T(8,128)(2,1)S(1)}, u32[]{:S(2)}, u32[]{:S(2)}) collective-permute-start(bf16[512,512]{1,0:T(8,128)(2,1)S(1)} %copy-done.12), channel_id=1, source_target_pairs={{0,24},{4,28},{8,0},{12,4},{16,8},{20,12},{24,16},{28,20},{1,25},{... | collective-permute-start | bytes 1572872 | tf_op jit(solution)/shard_map/ppermute | solution.py:23
  164.1 26.1 %collective-permute-start.29 = (bf16[512,512]{1,0:T(8,128)(2,1)S(1)}, bf16[512,512]{1,0:T(8,128)(2,1)S(1)}, u32[]{:S(2)}, u32[]{:S(2)}) collective-permute-start(bf16[512,512]{1,0:T(8,128)(2,1)S(1)} %copy-done.11), channel_id=1, source_target_pairs={{0,4},{4,0},{8,12},{12,8},{16,20},{20,16},{24,28},{28,24},{1,5},{5... | collective-permute-start | bytes 1572872 | tf_op jit(solution)/shard_map/ppermute | solution.py:23
  165.7 27.5 %collective-permute-start.10 = (bf16[512,512]{1,0:T(8,128)(2,1)S(1)}, bf16[512,512]{1,0:T(8,128)(2,1)S(1)}, u32[]{:S(2)}, u32[]{:S(2)}) collective-permute-start(bf16[512,512]{1,0:T(8,128)(2,1)S(1)} %copy-done.16), channel_id=1, source_target_pairs={{0,4},{4,0},{8,12},{12,8},{16,20},{20,16},{24,28},{28,24},{1,5},{5... | collective-permute-start | bytes 1572872 | tf_op jit(solution)/shard_map/ppermute | solution.py:23
  188.8 34.9 %collective-permute-start.15 = (bf16[384,1024]{1,0:T(8,128)(2,1)S(1)}, bf16[384,1024]{1,0:T(8,128)(2,1)S(1)}, u32[]{:S(2)}, u32[]{:S(2)}) collective-permute-start(bf16[384,1024]{1,0:T(8,128)(2,1)S(1)} %broadcast_select_fusion.1), channel_id=1, source_target_pairs={{0,2},{2,0},{1,3},{3,1},{4,6},{6,4},{5,7},{7,5},{8,10},{10,8},{9,1... | collective-permute-start | bytes 2359304 | tf_op jit(solution)/shard_map/ppermute | solution.py:30
  190.2 32.6 %collective-permute-start.14 = (bf16[384,1024]{1,0:T(8,128)(2,1)S(1)}, bf16[384,1024]{1,0:T(8,128)(2,1)S(1)}, u32[]{:S(2)}, u32[]{:S(2)}) collective-permute-start(bf16[384,1024]{1,0:T(8,128)(2,1)S(1)} %broadcast_select_fusion.2), channel_id=1, source_target_pairs={{0,2},{2,0},{1,3},{3,1},{4,6},{6,4},{5,7},{7,5},{8,10},{10,8},{9,1... | collective-permute-start | bytes 2359304 | tf_op jit(solution)/shard_map/ppermute | solution.py:30
  191.7 39.6 %collective-permute-start.16 = (bf16[384,1024]{1,0:T(8,128)(2,1)S(1)}, bf16[384,1024]{1,0:T(8,128)(2,1)S(1)}, u32[]{:S(2)}, u32[]{:S(2)}) collective-permute-start(bf16[384,1024]{1,0:T(8,128)(2,1)S(1)} %broadcast_select_fusion), channel_id=1, source_target_pairs={{0,2},{2,0},{1,3},{3,1},{4,6},{6,4},{5,7},{7,5},{8,10},{10,8},{9,1... | collective-permute-start | bytes 2359304 | tf_op jit(solution)/shard_map/ppermute | solution.py:30
  193.2 91.5 %collective-permute-start.17 = (bf16[1536,1024]{1,0:T(8,128)(2,1)S(1)}, bf16[1536,1024]{1,0:T(8,128)(2,1)S(1)}, u32[]{:S(2)}, u32[]{:S(2)}) collective-permute-start(bf16[1536,1024]{1,0:T(8,128)(2,1)S(1)} %pad_maximum_fusion), channel_id=1, source_target_pairs={{0,1},{1,0},{2,3},{3,2},{4,5},{5,4},{6,7},{7,6},{8,9},{9,8},{10,11... | collective-permute-start | bytes 9437192 | tf_op jit(solution)/shard_map/ppermute | solution.py:30
  195.9 36.3 %collective-permute-start.12 = (bf16[512,512]{1,0:T(8,128)(2,1)}, bf16[512,512]{1,0:T(8,128)(2,1)S(1)}, u32[]{:S(2)}, u32[]{:S(2)}) collective-permute-start(bf16[512,512]{1,0:T(8,128)(2,1)} %collective-permute-done.8), channel_id=1, source_target_pairs={{0,4},{4,0},{8,12},{12,8},{16,20},{20,16},{24,28},{28,24},{1,5},{5... | collective-permute-start | bytes 1572872 | tf_op jit(solution)/shard_map/ppermute | solution.py:23
  231.2 22.0 %collective-permute-start.25 = (bf16[512,512]{1,0:T(8,128)(2,1)S(1)}, bf16[512,512]{1,0:T(8,128)(2,1)S(1)}, u32[]{:S(2)}, u32[]{:S(2)}) collective-permute-start(bf16[512,512]{1,0:T(8,128)(2,1)S(1)} %collective-permute-done.21), channel_id=1, source_target_pairs={{0,4},{4,0},{8,12},{12,8},{16,20},{20,16},{24,28},{28,24},{1,5},{5... | collective-permute-start | bytes 1572872 | tf_op jit(solution)/shard_map/ppermute | solution.py:23
  232.1 57.8 %collective-permute-start.18 = (bf16[1536,1024]{1,0:T(8,128)(2,1)S(1)}, bf16[1536,1024]{1,0:T(8,128)(2,1)S(1)}, u32[]{:S(2)}, u32[]{:S(2)}) collective-permute-start(bf16[1536,1024]{1,0:T(8,128)(2,1)S(1)} %constant_dynamic-update-slice_fusion.24), channel_id=1, source_target_pairs={{0,1},{1,0},{2,3},{3,2},{4,5},{5,4},{6,7},{7,6},{8,9},{9,8},{10,11... | collective-permute-start | bytes 9437192 | tf_op jit(solution)/shard_map/ppermute | solution.py:30
  233.5 31.0 %collective-permute-start.30 = (bf16[512,512]{1,0:T(8,128)(2,1)S(1)}, bf16[512,512]{1,0:T(8,128)(2,1)S(1)}, u32[]{:S(2)}, u32[]{:S(2)}) collective-permute-start(bf16[512,512]{1,0:T(8,128)(2,1)S(1)} %collective-permute-done.26), channel_id=1, source_target_pairs={{0,4},{4,0},{8,12},{12,8},{16,20},{20,16},{24,28},{28,24},{1,5},{5... | collective-permute-start | bytes 1572872 | tf_op jit(solution)/shard_map/ppermute | solution.py:23
  242.0 30.8 %collective-permute-start.31 = (bf16[512,512]{1,0:T(8,128)(2,1)S(1)}, bf16[512,512]{1,0:T(8,128)(2,1)S(1)}, u32[]{:S(2)}, u32[]{:S(2)}) collective-permute-start(bf16[512,512]{1,0:T(8,128)(2,1)S(1)} %collective-permute-done.27), channel_id=1, source_target_pairs={{0,4},{4,0},{8,12},{12,8},{16,20},{20,16},{24,28},{28,24},{1,5},{5... | collective-permute-start | bytes 1572872 | tf_op jit(solution)/shard_map/ppermute | solution.py:23
  253.2 25.2 %collective-permute-start.32 = (bf16[512,512]{1,0:T(8,128)(2,1)S(1)}, bf16[512,512]{1,0:T(8,128)(2,1)S(1)}, u32[]{:S(2)}, u32[]{:S(2)}) collective-permute-start(bf16[512,512]{1,0:T(8,128)(2,1)S(1)} %collective-permute-done.28), channel_id=1, source_target_pairs={{0,4},{4,0},{8,12},{12,8},{16,20},{20,16},{24,28},{28,24},{1,5},{5... | collective-permute-start | bytes 1572872 | tf_op jit(solution)/shard_map/ppermute | solution.py:23
  318.7 44.8 %collective-permute-start.35 = (bf16[384,2048]{1,0:T(8,128)(2,1)S(1)}, bf16[384,2048]{1,0:T(8,128)(2,1)S(1)}, u32[]{:S(2)}, u32[]{:S(2)}) collective-permute-start(bf16[384,2048]{1,0:T(8,128)(2,1)S(1)} %convolution_convert_fusion.4), channel_id=1, source_target_pairs={{0,1},{1,0},{2,3},{3,2},{4,5},{5,4},{6,7},{7,6},{8,9},{9,8},{10,11... | collective-permute-start | bytes 4718600 | tf_op jit(solution)/shard_map/ppermute | solution.py:30
  327.3 38.5 %collective-permute-start.38 = (bf16[384,1024]{1,0:T(8,128)(2,1)S(1)}, bf16[384,1024]{1,0:T(8,128)(2,1)S(1)}, u32[]{:S(2)}, u32[]{:S(2)}) collective-permute-start(bf16[384,1024]{1,0:T(8,128)(2,1)S(1)} %slice.125), channel_id=1, source_target_pairs={{0,2},{2,0},{1,3},{3,1},{4,6},{6,4},{5,7},{7,5},{8,10},{10,8},{9,1... | collective-permute-start | bytes 2359304 | tf_op jit(solution)/shard_map/ppermute | solution.py:30
  342.9 33.9 %collective-permute-start.41 = (bf16[384,1024]{1,0:T(8,128)(2,1)S(1)}, bf16[384,1024]{1,0:T(8,128)(2,1)S(1)}, u32[]{:S(2)}, u32[]{:S(2)}) collective-permute-start(bf16[384,1024]{1,0:T(8,128)(2,1)S(1)} %fusion.10), channel_id=1, source_target_pairs={{0,8},{4,12},{1,9},{5,13},{2,10},{6,14},{3,11},{7,15}} | collective-permute-start | bytes 2359304 | tf_op jit(solution)/shard_map/ppermute | solution.py:27
  412.4 42.2 %collective-permute-start.46 = (bf16[384,1024]{1,0:T(8,128)(2,1)}, bf16[384,1024]{1,0:T(8,128)(2,1)}, u32[]{:S(2)}, u32[]{:S(2)}) collective-permute-start(bf16[384,1024]{1,0:T(8,128)(2,1)} %add_convert_fusion.5), channel_id=1, source_target_pairs={{8,0},{12,4},{16,8},{20,12},{24,16},{28,20},{9,1},{13,5},{17,9},{2... | collective-permute-start | bytes 2359304 | tf_op jit(solution)/shard_map/ppermute | solution.py:27
  (35 other events, 972.8 us)

commit v3 on v1

--- a/solution.py
+++ b/solution.py
@@ -20,6 +20,10 @@
         for a in range(ring):
             for b in range(span):
                 pairs.append((a * span + b, ((a + step_a) % ring) * span + (b + step_b) % span))
+        return lax.ppermute(value, "fsdp", pairs)
+
+    def send_line(value, senders, step):
+        pairs = [(a * span + b, (a + step) * span + b) for a in senders for b in range(span)]
         return lax.ppermute(value, "fsdp", pairs)
 
     def send_axis(value, axis, count, step):
@@ -67,7 +71,14 @@
         gate_full = move_weight(gate_weight, 1)
         up_full = move_weight(up_weight, 1)
         down_full = move_weight(down_weight, 0)
-        slots = [normed] + [send_f(normed, k, 0) for k in range(1, ring)]
+        a = lax.axis_index("fsdp") // span
+        rightward, leftward = [normed], [normed]
+        for k in range(1, ring):
+            rightward.append(send_line(rightward[-1], range(k - 1, ring - 1), 1))
+            leftward.append(send_line(leftward[-1], range(1, ring - k + 1), -1))
+        slots = [normed] + [
+            jnp.where(a >= k, rightward[k], leftward[ring - k]) for k in range(1, ring)
+        ]
         columns = [jnp.concatenate(slots, axis=0)]
         for step in range(1, count_t):
             moved = [send_axis(piece, "tensor", count_t, -step) for piece in slots]

time: 457 us -> 453 us (level); the launches traced: 456 us -> 447 us
  waiting for transfers between devices: 200 us -> 186 us
  matrix products: 47.3 us -> 53.7 us
    ppermute x27 -> x24, starting transfers between devices: 136 us -> 121 us  [send_f(): return lax.ppermute(value, 'fsdp', pairs)]
    ppermute x27 -> x24, waiting for transfers between devices: 135 us -> 122 us  [send_f(): return lax.ppermute(value, 'fsdp', pairs)]
    ppermute x14, waiting for transfers between devices: 64.5 us -> 51.6 us  [send_axis(): lax.ppermute(value, axis, [(i, (i + step) % count) for i in range(count)])]
    ppermute x0 -> x6, waiting for transfers between devices: none -> 11.6 us  [send_line(): return lax.ppermute(value, 'fsdp', pairs)]
    ppermute x0 -> x6, starting transfers between devices: none -> 10.8 us  [send_line(): return lax.ppermute(value, 'fsdp', pairs)]
    dot_general x8, matrix products: 26 us -> 31.3 us  [block_update(): jnp.dot(piece, weight[k * width:(k + 1) * width], preferred_element_type=...]
  transfers between devices with their start and end apart: 41 -> 44, of which waited for: 16 -> 18; matrix products, arithmetic and copies ran while one was open for 14% -> 14% of each run, Pallas kernels for 0% -> 0%
where the time goes in v3:
time: 453 us; the launch traced here: 447 us
  waiting for transfers between devices  186 us (41%)
  starting transfers between devices  143 us (32%)
  matrix products  53.7 us (12%)
  local copies, waits for them, and re-layouts  40.6 us (9%)
  other arithmetic  15.2 us (3%)
  blocking collectives  8.41 us (2%)
    ppermute x24, waiting for transfers between devices, send_f(): return lax.ppermute(value, 'fsdp', pairs)  122 us
    ppermute x24, starting transfers between devices, send_f(): return lax.ppermute(value, 'fsdp', pairs)  121 us
    ppermute x14, waiting for transfers between devices, send_axis(): lax.ppermute(value, axis, [(i, (i + step) % count) for i in range(count)])  51.6 us
    dot_general x8, matrix products, block_update(): jnp.dot(piece, weight[k * width:(k + 1) * width], preferred_element_type=...  31.3 us
    dot_general x8, matrix products, block_update(): jnp.dot(part, down_full[:, k * half:(k + 1) * half], preferred_element_ty...  20.6 us
    dynamic_update_slice x21, local copies, waits for them, and re-layouts, move_weight(): lax.dynamic_update_slice_in_dim(whole, piece, place(owner) * width, join_...  17.6 us
    ppermute x6, waiting for transfers between devices, send_line(): return lax.ppermute(value, 'fsdp', pairs)  11.6 us
    ppermute x6, starting transfers between devices, send_line(): return lax.ppermute(value, 'fsdp', pairs)  10.8 us
  transfers between devices with their start and end apart: 44, of which 18 were waited for; matrix products, arithmetic and copies ran while one was open for 14% of the time, Pallas kernels for 0%

profile of v3, /device:TPU:0, one launch (start us, length us, event | category | flops | bytes accessed | tf_op | source)
XLA Modules:
  0.0 447.1 jit_solution(9448130566980574692)
XLA Ops:
  3.5 8.4 %psum.7 = f32[384,1]{0,1:T(1,128)S(1)} all-reduce(f32[384,1]{0,1:T(1,128)S(1)} %broadcast_in_dim.34), channel_id=1, replica_groups=mesh['fsdp'=8,'tensor'=2,'dp'=2] {'tensor','dp'}, use_global_device_ids=true, to_apply=%region_3.4 | all-reduce | flops 384 | bytes 3072 | tf_op jit(solution)/shard_map/psum | solution.py:66
  14.1 4.6 %collective-permute-start = (bf16[384,1024]{1,0:T(8,128)(2,1)S(1)}, bf16[384,1024]{1,0:T(8,128)(2,1)S(1)}, u32[]{:S(2)}, u32[]{:S(2)}) collective-permute-start(bf16[384,1024]{1,0:T(8,128)(2,1)S(1)} %fusion.8), channel_id=1, source_target_pairs={{0,8},{4,12},{8,16},{12,20},{16,24},{20,28},{1,9},{5,13},{9,17},{1... | collective-permute-start | bytes 2359304 | tf_op jit(solution)/shard_map/ppermute | solution.py:27
  24.4 11.6 %collective-permute-done.1 = bf16[384,1024]{1,0:T(8,128)(2,1)S(1)} collective-permute-done((bf16[384,1024]{1,0:T(8,128)(2,1)S(1)}, bf16[384,1024]{1,0:T(8,128)(2,1)S(1)}, u32[]{:S(2)}, u32[]{:S(2)}) %collective-permute-start.1) | collective-permute-done | bytes 786464 | tf_op jit(solution)/shard_map/ppermute | solution.py:27
  41.0 40.7 %collective-permute-start.19 = (bf16[512,512]{1,0:T(8,128)(2,1)}, bf16[512,512]{1,0:T(8,128)(2,1)}, u32[]{:S(2)}, u32[]{:S(2)}) collective-permute-start(bf16[512,512]{1,0:T(8,128)(2,1)} %get-tuple-element.21), channel_id=1, source_target_pairs={{0,8},{4,12},{8,16},{12,20},{16,24},{20,28},{24,0},{28,4},{1,9},{5... | collective-permute-start | bytes 1572872 | tf_op jit(solution)/shard_map/ppermute | solution.py:23
  94.3 8.0 %collective-permute-start.21 = (bf16[512,512]{1,0:T(8,128)(2,1)}, bf16[512,512]{1,0:T(8,128)(2,1)S(1)}, u32[]{:S(2)}, u32[]{:S(2)}) collective-permute-start(bf16[512,512]{1,0:T(8,128)(2,1)} %get-tuple-element.20), channel_id=1, source_target_pairs={{0,24},{4,28},{8,0},{12,4},{16,8},{20,12},{24,16},{28,20},{1,25},{... | collective-permute-start | bytes 1572872 | tf_op jit(solution)/shard_map/ppermute | solution.py:23
  104.1 16.5 %collective-permute-done.20 = bf16[512,512]{1,0:T(8,128)(2,1)} collective-permute-done((bf16[512,512]{1,0:T(8,128)(2,1)}, bf16[512,512]{1,0:T(8,128)(2,1)}, u32[]{:S(2)}, u32[]{:S(2)}) %collective-permute-start.20) | collective-permute-done | bytes 524320 | tf_op jit(solution)/shard_map/ppermute | solution.py:23
  131.6 11.4 %collective-permute-done.21 = bf16[512,512]{1,0:T(8,128)(2,1)S(1)} collective-permute-done((bf16[512,512]{1,0:T(8,128)(2,1)}, bf16[512,512]{1,0:T(8,128)(2,1)S(1)}, u32[]{:S(2)}, u32[]{:S(2)}) %collective-permute-start.21) | collective-permute-done | bytes 524320 | tf_op jit(solution)/shard_map/ppermute | solution.py:23
  143.0 3.8 collective-permute-start.26
  154.4 4.7 %collective-permute-done.26 = bf16[512,512]{1,0:T(8,128)(2,1)S(1)} collective-permute-done((bf16[512,512]{1,0:T(8,128)(2,1)S(1)}, bf16[512,512]{1,0:T(8,128)(2,1)S(1)}, u32[]{:S(2)}, u32[]{:S(2)}) %collective-permute-start.26) | collective-permute-done | bytes 524320 | tf_op jit(solution)/shard_map/ppermute | solution.py:23
  159.1 5.0 %collective-permute-start.28 = (bf16[512,512]{1,0:T(8,128)(2,1)S(1)}, bf16[512,512]{1,0:T(8,128)(2,1)S(1)}, u32[]{:S(2)}, u32[]{:S(2)}) collective-permute-start(bf16[512,512]{1,0:T(8,128)(2,1)S(1)} %copy-done.11), channel_id=1, source_target_pairs={{0,24},{4,28},{8,0},{12,4},{16,8},{20,12},{24,16},{28,20},{1,25},{... | collective-permute-start | bytes 1572872 | tf_op jit(solution)/shard_map/ppermute | solution.py:23
  166.4 10.5 %collective-permute-done.27 = bf16[512,512]{1,0:T(8,128)(2,1)S(1)} collective-permute-done((bf16[512,512]{1,0:T(8,128)(2,1)S(1)}, bf16[512,512]{1,0:T(8,128)(2,1)S(1)}, u32[]{:S(2)}, u32[]{:S(2)}) %collective-permute-start.27) | collective-permute-done | bytes 524320 | tf_op jit(solution)/shard_map/ppermute | solution.py:23
  178.5 10.3 %collective-permute-done.28 = bf16[512,512]{1,0:T(8,128)(2,1)S(1)} collective-permute-done((bf16[512,512]{1,0:T(8,128)(2,1)S(1)}, bf16[512,512]{1,0:T(8,128)(2,1)S(1)}, u32[]{:S(2)}, u32[]{:S(2)}) %collective-permute-start.28) | collective-permute-done | bytes 524320 | tf_op jit(solution)/shard_map/ppermute | solution.py:23
  197.1 25.7 %collective-permute-done.14 = bf16[384,1024]{1,0:T(8,128)(2,1)S(1)} collective-permute-done((bf16[384,1024]{1,0:T(8,128)(2,1)S(1)}, bf16[384,1024]{1,0:T(8,128)(2,1)S(1)}, u32[]{:S(2)}, u32[]{:S(2)}) %collective-permute-start.14) | collective-permute-done | bytes 786464 | tf_op jit(solution)/shard_map/ppermute | solution.py:30
  225.1 6.2 %collective-permute-done.16 = bf16[384,1024]{1,0:T(8,128)(2,1)S(1)} collective-permute-done((bf16[384,1024]{1,0:T(8,128)(2,1)S(1)}, bf16[384,1024]{1,0:T(8,128)(2,1)S(1)}, u32[]{:S(2)}, u32[]{:S(2)}) %collective-permute-start.16) | collective-permute-done | bytes 786464 | tf_op jit(solution)/shard_map/ppermute | solution.py:30
  234.5 7.7 %collective-permute-done.24 = bf16[512,512]{1,0:T(8,128)(2,1)S(1)} collective-permute-done((bf16[512,512]{1,0:T(8,128)(2,1)}, bf16[512,512]{1,0:T(8,128)(2,1)S(1)}, u32[]{:S(2)}, u32[]{:S(2)}) %collective-permute-start.24) | collective-permute-done | bytes 524320 | tf_op jit(solution)/shard_map/ppermute | solution.py:23
  242.2 11.2 %collective-permute-done.25 = bf16[512,512]{1,0:T(8,128)(2,1)S(1)} collective-permute-done((bf16[512,512]{1,0:T(8,128)(2,1)S(1)}, bf16[512,512]{1,0:T(8,128)(2,1)S(1)}, u32[]{:S(2)}, u32[]{:S(2)}) %collective-permute-start.25) | collective-permute-done | bytes 524320 | tf_op jit(solution)/shard_map/ppermute | solution.py:23
  253.6 11.1 %collective-permute-done.30 = bf16[512,512]{1,0:T(8,128)(2,1)S(1)} collective-permute-done((bf16[512,512]{1,0:T(8,128)(2,1)S(1)}, bf16[512,512]{1,0:T(8,128)(2,1)S(1)}, u32[]{:S(2)}, u32[]{:S(2)}) %collective-permute-start.30) | collective-permute-done | bytes 524320 | tf_op jit(solution)/shard_map/ppermute | solution.py:23
  265.5 7.4 %collective-permute-done.31 = bf16[512,512]{1,0:T(8,128)(2,1)S(1)} collective-permute-done((bf16[512,512]{1,0:T(8,128)(2,1)S(1)}, bf16[512,512]{1,0:T(8,128)(2,1)S(1)}, u32[]{:S(2)}, u32[]{:S(2)}) %collective-permute-start.31) | collective-permute-done | bytes 524320 | tf_op jit(solution)/shard_map/ppermute | solution.py:23
  273.8 4.7 %collective-permute-done.32 = bf16[512,512]{1,0:T(8,128)(2,1)S(1)} collective-permute-done((bf16[512,512]{1,0:T(8,128)(2,1)S(1)}, bf16[512,512]{1,0:T(8,128)(2,1)S(1)}, u32[]{:S(2)}, u32[]{:S(2)}) %collective-permute-start.32) | collective-permute-done | bytes 524320 | tf_op jit(solution)/shard_map/ppermute | solution.py:23
  281.2 3.5 fusion.22
  289.9 3.4 fusion.25
  293.4 6.9 %fusion.4 = f32[1536,512]{1,0:T(8,128)S(1)} fusion(f32[1536,512]{1,0:T(8,128)} %fusion.25, f32[1536,512]{1,0:T(8,128)S(1)} %fusion.27, f32[1536,512]{1,0:T(8,128)S(1)} %fusion.29, bf16[4096,512]{1,0:T(8,128)(2,1)S(1)} %constant_dynamic-update-slice_fusion.16, bf16[384,1024]{1,0:T(8,128)(2,1)S(1)} %broadcast_select_fusion, ...), kind=kOutput, calls=%fused_computation.8 | convolution fusion | flops 1625554944 | bytes 16777216 | tf_op jit(solution)/shard_map/dot_general | solution.py:90
  300.3 3.4 fusion.18
  303.7 6.9 %fusion.5 = bf16[1536,512]{1,0:T(8,128)(2,1)S(1)} fusion(f32[1536,512]{1,0:T(8,128)} %fusion.18, f32[1536,512]{1,0:T(8,128)S(1)} %copy-done.18, f32[1536,512]{1,0:T(8,128)S(1)} %copy-done.17, f32[1536,512]{1,0:T(8,128)S(1)} %fusion.4, bf16[4096,512]{1,0:T(8,128)(2,1)S(1)} %constant_dynamic-update-slice_fusion.8, ...), kind=kOutput, calls=%fused_computation.14 | convolution fusion | flops 1630273536 | bytes 18350080 | tf_op jit(solution)/shard_map/dot_general | solution.py:90
  339.9 13.9 %collective-permute-done.34 = bf16[384,1024]{1,0:T(8,128)(2,1)S(1)} collective-permute-done((bf16[384,1024]{1,0:T(8,128)(2,1)S(1)}, bf16[384,1024]{1,0:T(8,128)(2,1)S(1)}, u32[]{:S(2)}, u32[]{:S(2)}) %collective-permute-start.34) | collective-permute-done | bytes 786464 | tf_op jit(solution)/shard_map/ppermute | solution.py:30
  354.1 18.2 %collective-permute-start.35 = (bf16[384,1024]{1,0:T(8,128)(2,1)S(1)}, bf16[384,1024]{1,0:T(8,128)(2,1)}, u32[]{:S(2)}, u32[]{:S(2)}) collective-permute-start(bf16[384,1024]{1,0:T(8,128)(2,1)S(1)} %add_convert_fusion.7), channel_id=1, source_target_pairs={{0,24},{4,28},{8,0},{12,4},{16,8},{20,12},{24,16},{28,20},{1,25},{... | collective-permute-start | bytes 2359304 | tf_op jit(solution)/shard_map/ppermute | solution.py:23
  372.6 9.1 %collective-permute-start.38 = (bf16[384,1024]{1,0:T(8,128)(2,1)S(1)}, bf16[384,1024]{1,0:T(8,128)(2,1)}, u32[]{:S(2)}, u32[]{:S(2)}) collective-permute-start(bf16[384,1024]{1,0:T(8,128)(2,1)S(1)} %add_convert_fusion.6), channel_id=1, source_target_pairs={{0,16},{4,20},{8,24},{12,28},{16,0},{20,4},{24,8},{28,12},{1,17},{... | collective-permute-start | bytes 2359304 | tf_op jit(solution)/shard_map/ppermute | solution.py:23
  381.7 5.8 %collective-permute-done.40 = bf16[384,1024]{1,0:T(8,128)(2,1)S(1)} collective-permute-done((bf16[384,1024]{1,0:T(8,128)(2,1)S(1)}, bf16[384,1024]{1,0:T(8,128)(2,1)S(1)}, u32[]{:S(2)}, u32[]{:S(2)}) %collective-permute-start.40) | collective-permute-done | bytes 786464 | tf_op jit(solution)/shard_map/ppermute | solution.py:30
  388.7 15.8 %collective-permute-start.41 = (bf16[384,1024]{1,0:T(8,128)(2,1)}, bf16[384,1024]{1,0:T(8,128)(2,1)}, u32[]{:S(2)}, u32[]{:S(2)}) collective-permute-start(bf16[384,1024]{1,0:T(8,128)(2,1)} %add_convert_fusion.5), channel_id=1, source_target_pairs={{0,8},{4,12},{8,16},{12,20},{16,24},{20,28},{24,0},{28,4},{1,9},{5... | collective-permute-start | bytes 2359304 | tf_op jit(solution)/shard_map/ppermute | solution.py:23
  404.5 8.1 %gather_fusion.1 = bf16[512,1024]{1,0:T(8,128)(2,1)} fusion(bf16[8,64,1024]{2,1,0:T(8,128)(2,1)S(1)} %bitcast.19, s32[512]{0:T(512)S(1)} %reshape.108), kind=kCustom, calls=%fused_computation.1 | custom fusion | bytes 2101248 | tf_op jit(solution)/shard_map/vmap()/gather | solution.py:137
  412.7 25.1 %collective-permute-done.38 = bf16[384,1024]{1,0:T(8,128)(2,1)} collective-permute-done((bf16[384,1024]{1,0:T(8,128)(2,1)S(1)}, bf16[384,1024]{1,0:T(8,128)(2,1)}, u32[]{:S(2)}, u32[]{:S(2)}) %collective-permute-start.38) | collective-permute-done | bytes 786464 | tf_op jit(solution)/shard_map/ppermute | solution.py:23
  443.3 3.6 fusion.17
  (179 shorter events, 113.0 us)
Async XLA Ops:
  12.8 23.2 %collective-permute-start.1 = (bf16[384,1024]{1,0:T(8,128)(2,1)S(1)}, bf16[384,1024]{1,0:T(8,128)(2,1)S(1)}, u32[]{:S(2)}, u32[]{:S(2)}) collective-permute-start(bf16[384,1024]{1,0:T(8,128)(2,1)S(1)} %fusion.8), channel_id=1, source_target_pairs={{8,0},{12,4},{16,8},{20,12},{24,16},{28,20},{9,1},{13,5},{17,9},{2... | collective-permute-start | bytes 2359304 | tf_op jit(solution)/shard_map/ppermute | solution.py:27
  14.1 70.6 %collective-permute-start = (bf16[384,1024]{1,0:T(8,128)(2,1)S(1)}, bf16[384,1024]{1,0:T(8,128)(2,1)S(1)}, u32[]{:S(2)}, u32[]{:S(2)}) collective-permute-start(bf16[384,1024]{1,0:T(8,128)(2,1)S(1)} %fusion.8), channel_id=1, source_target_pairs={{0,8},{4,12},{8,16},{12,20},{16,24},{20,28},{1,9},{5,13},{9,17},{1... | collective-permute-start | bytes 2359304 | tf_op jit(solution)/shard_map/ppermute | solution.py:27
  21.7 59.9 %collective-permute-start.6 = (bf16[512,512]{1,0:T(8,128)(2,1)S(1)}, bf16[512,512]{1,0:T(8,128)(2,1)S(1)}, u32[]{:S(2)}, u32[]{:S(2)}) collective-permute-start(bf16[512,512]{1,0:T(8,128)(2,1)S(1)} %get-tuple-element.16), channel_id=1, source_target_pairs={{0,8},{4,12},{8,16},{12,20},{16,24},{20,28},{24,0},{28,4},{1,9},{5... | collective-permute-start | bytes 1572872 | tf_op jit(solution)/shard_map/ppermute | solution.py:23
  23.3 67.3 %collective-permute-start.7 = (bf16[512,512]{1,0:T(8,128)(2,1)}, bf16[512,512]{1,0:T(8,128)(2,1)}, u32[]{:S(2)}, u32[]{:S(2)}) collective-permute-start(bf16[512,512]{1,0:T(8,128)(2,1)} %get-tuple-element.19), channel_id=1, source_target_pairs={{0,16},{4,20},{8,24},{12,28},{16,0},{20,4},{24,8},{28,12},{1,17},{... | collective-permute-start | bytes 1572872 | tf_op jit(solution)/shard_map/ppermute | solution.py:23
  36.0 88.0 %collective-permute-start.2 = (bf16[384,1024]{1,0:T(8,128)(2,1)S(1)}, bf16[384,1024]{1,0:T(8,128)(2,1)}, u32[]{:S(2)}, u32[]{:S(2)}) collective-permute-start(bf16[384,1024]{1,0:T(8,128)(2,1)S(1)} %collective-permute-done.1), channel_id=1, source_target_pairs={{8,0},{12,4},{16,8},{20,12},{9,1},{13,5},{17,9},{21,13},{10,2},{14... | collective-permute-start | bytes 2359304 | tf_op jit(solution)/shard_map/ppermute | solution.py:27
  41.0 53.3 %collective-permute-start.19 = (bf16[512,512]{1,0:T(8,128)(2,1)}, bf16[512,512]{1,0:T(8,128)(2,1)}, u32[]{:S(2)}, u32[]{:S(2)}) collective-permute-start(bf16[512,512]{1,0:T(8,128)(2,1)} %get-tuple-element.21), channel_id=1, source_target_pairs={{0,8},{4,12},{8,16},{12,20},{16,24},{20,28},{24,0},{28,4},{1,9},{5... | collective-permute-start | bytes 1572872 | tf_op jit(solution)/shard_map/ppermute | solution.py:23
  82.5 38.2 %collective-permute-start.20 = (bf16[512,512]{1,0:T(8,128)(2,1)}, bf16[512,512]{1,0:T(8,128)(2,1)}, u32[]{:S(2)}, u32[]{:S(2)}) collective-permute-start(bf16[512,512]{1,0:T(8,128)(2,1)} %get-tuple-element.24), channel_id=1, source_target_pairs={{0,16},{4,20},{8,24},{12,28},{16,0},{20,4},{24,8},{28,12},{1,17},{... | collective-permute-start | bytes 1572872 | tf_op jit(solution)/shard_map/ppermute | solution.py:23
  84.8 62.0 %collective-permute-start.4 = (bf16[384,1024]{1,0:T(8,128)(2,1)S(1)}, bf16[384,1024]{1,0:T(8,128)(2,1)}, u32[]{:S(2)}, u32[]{:S(2)}) collective-permute-start(bf16[384,1024]{1,0:T(8,128)(2,1)S(1)} %collective-permute-done), channel_id=1, source_target_pairs={{8,16},{12,20},{16,24},{20,28},{9,17},{13,21},{17,25},{21,29},{10,... | collective-permute-start | bytes 2359304 | tf_op jit(solution)/shard_map/ppermute | solution.py:27
  90.5 38.7 %collective-permute-start.8 = (bf16[512,512]{1,0:T(8,128)(2,1)}, bf16[512,512]{1,0:T(8,128)(2,1)}, u32[]{:S(2)}, u32[]{:S(2)}) collective-permute-start(bf16[512,512]{1,0:T(8,128)(2,1)} %get-tuple-element.15), channel_id=1, source_target_pairs={{0,24},{4,28},{8,0},{12,4},{16,8},{20,12},{24,16},{28,20},{1,25},{... | collective-permute-start | bytes 1572872 | tf_op jit(solution)/shard_map/ppermute | solution.py:23
  94.3 48.8 %collective-permute-start.21 = (bf16[512,512]{1,0:T(8,128)(2,1)}, bf16[512,512]{1,0:T(8,128)(2,1)S(1)}, u32[]{:S(2)}, u32[]{:S(2)}) collective-permute-start(bf16[512,512]{1,0:T(8,128)(2,1)} %get-tuple-element.20), channel_id=1, source_target_pairs={{0,24},{4,28},{8,0},{12,4},{16,8},{20,12},{24,16},{28,20},{1,25},{... | collective-permute-start | bytes 1572872 | tf_op jit(solution)/shard_map/ppermute | solution.py:23
  120.6 27.7 %collective-permute-start.9 = (bf16[512,512]{1,0:T(8,128)(2,1)}, bf16[512,512]{1,0:T(8,128)(2,1)S(1)}, u32[]{:S(2)}, u32[]{:S(2)}) collective-permute-start(bf16[512,512]{1,0:T(8,128)(2,1)} %get-tuple-element.18), channel_id=1, source_target_pairs={{0,4},{4,0},{8,12},{12,8},{16,20},{20,16},{24,28},{28,24},{1,5},{5... | collective-permute-start | bytes 1572872 | tf_op jit(solution)/shard_map/ppermute | solution.py:23
  124.0 40.1 %collective-permute-start.3 = (bf16[384,1024]{1,0:T(8,128)(2,1)}, bf16[384,1024]{1,0:T(8,128)(2,1)S(1)}, u32[]{:S(2)}, u32[]{:S(2)}) collective-permute-start(bf16[384,1024]{1,0:T(8,128)(2,1)} %collective-permute-done.2), channel_id=1, source_target_pairs={{8,0},{12,4},{9,1},{13,5},{10,2},{14,6},{11,3},{15,7}} | collective-permute-start | bytes 2359304 | tf_op jit(solution)/shard_map/ppermute | solution.py:27
  148.3 43.1 %collective-permute-start.13 = (bf16[384,1024]{1,0:T(8,128)(2,1)S(1)}, bf16[384,1024]{1,0:T(8,128)(2,1)S(1)}, u32[]{:S(2)}, u32[]{:S(2)}) collective-permute-start(bf16[384,1024]{1,0:T(8,128)(2,1)S(1)} %fusion.8), channel_id=1, source_target_pairs={{0,2},{2,0},{1,3},{3,1},{4,6},{6,4},{5,7},{7,5},{8,10},{10,8},{9,1... | collective-permute-start | bytes 2359304 | tf_op jit(solution)/shard_map/ppermute | solution.py:30
  152.1 24.9 %collective-permute-start.27 = (bf16[512,512]{1,0:T(8,128)(2,1)S(1)}, bf16[512,512]{1,0:T(8,128)(2,1)S(1)}, u32[]{:S(2)}, u32[]{:S(2)}) collective-permute-start(bf16[512,512]{1,0:T(8,128)(2,1)S(1)} %copy-done.12), channel_id=1, source_target_pairs={{0,16},{4,20},{8,24},{12,28},{16,0},{20,4},{24,8},{28,12},{1,17},{... | collective-permute-start | bytes 1572872 | tf_op jit(solution)/shard_map/ppermute | solution.py:23
  159.1 29.7 %collective-permute-start.28 = (bf16[512,512]{1,0:T(8,128)(2,1)S(1)}, bf16[512,512]{1,0:T(8,128)(2,1)S(1)}, u32[]{:S(2)}, u32[]{:S(2)}) collective-permute-start(bf16[512,512]{1,0:T(8,128)(2,1)S(1)} %copy-done.11), channel_id=1, source_target_pairs={{0,24},{4,28},{8,0},{12,4},{16,8},{20,12},{24,16},{28,20},{1,25},{... | collective-permute-start | bytes 1572872 | tf_op jit(solution)/shard_map/ppermute | solution.py:23
  164.1 26.2 %collective-permute-start.29 = (bf16[512,512]{1,0:T(8,128)(2,1)S(1)}, bf16[512,512]{1,0:T(8,128)(2,1)S(1)}, u32[]{:S(2)}, u32[]{:S(2)}) collective-permute-start(bf16[512,512]{1,0:T(8,128)(2,1)S(1)} %copy-done.10), channel_id=1, source_target_pairs={{0,4},{4,0},{8,12},{12,8},{16,20},{20,16},{24,28},{28,24},{1,5},{5... | collective-permute-start | bytes 1572872 | tf_op jit(solution)/shard_map/ppermute | solution.py:23
  165.7 27.3 %collective-permute-start.10 = (bf16[512,512]{1,0:T(8,128)(2,1)S(1)}, bf16[512,512]{1,0:T(8,128)(2,1)S(1)}, u32[]{:S(2)}, u32[]{:S(2)}) collective-permute-start(bf16[512,512]{1,0:T(8,128)(2,1)S(1)} %copy-done.15), channel_id=1, source_target_pairs={{0,4},{4,0},{8,12},{12,8},{16,20},{20,16},{24,28},{28,24},{1,5},{5... | collective-permute-start | bytes 1572872 | tf_op jit(solution)/shard_map/ppermute | solution.py:23
  188.8 34.8 %collective-permute-start.15 = (bf16[384,1024]{1,0:T(8,128)(2,1)S(1)}, bf16[384,1024]{1,0:T(8,128)(2,1)S(1)}, u32[]{:S(2)}, u32[]{:S(2)}) collective-permute-start(bf16[384,1024]{1,0:T(8,128)(2,1)S(1)} %broadcast_select_fusion.1), channel_id=1, source_target_pairs={{0,2},{2,0},{1,3},{3,1},{4,6},{6,4},{5,7},{7,5},{8,10},{10,8},{9,1... | collective-permute-start | bytes 2359304 | tf_op jit(solution)/shard_map/ppermute | solution.py:30
  190.3 32.6 %collective-permute-start.14 = (bf16[384,1024]{1,0:T(8,128)(2,1)S(1)}, bf16[384,1024]{1,0:T(8,128)(2,1)S(1)}, u32[]{:S(2)}, u32[]{:S(2)}) collective-permute-start(bf16[384,1024]{1,0:T(8,128)(2,1)S(1)} %broadcast_select_fusion.2), channel_id=1, source_target_pairs={{0,2},{2,0},{1,3},{3,1},{4,6},{6,4},{5,7},{7,5},{8,10},{10,8},{9,1... | collective-permute-start | bytes 2359304 | tf_op jit(solution)/shard_map/ppermute | solution.py:30
  191.5 39.8 %collective-permute-start.16 = (bf16[384,1024]{1,0:T(8,128)(2,1)S(1)}, bf16[384,1024]{1,0:T(8,128)(2,1)S(1)}, u32[]{:S(2)}, u32[]{:S(2)}) collective-permute-start(bf16[384,1024]{1,0:T(8,128)(2,1)S(1)} %broadcast_select_fusion), channel_id=1, source_target_pairs={{0,2},{2,0},{1,3},{3,1},{4,6},{6,4},{5,7},{7,5},{8,10},{10,8},{9,1... | collective-permute-start | bytes 2359304 | tf_op jit(solution)/shard_map/ppermute | solution.py:30
  193.0 91.7 %collective-permute-start.17 = (bf16[1536,1024]{1,0:T(8,128)(2,1)S(1)}, bf16[1536,1024]{1,0:T(8,128)(2,1)S(1)}, u32[]{:S(2)}, u32[]{:S(2)}) collective-permute-start(bf16[1536,1024]{1,0:T(8,128)(2,1)S(1)} %pad_maximum_fusion), channel_id=1, source_target_pairs={{0,1},{1,0},{2,3},{3,2},{4,5},{5,4},{6,7},{7,6},{8,9},{9,8},{10,11... | collective-permute-start | bytes 9437192 | tf_op jit(solution)/shard_map/ppermute | solution.py:30
  195.6 36.4 %collective-permute-start.12 = (bf16[512,512]{1,0:T(8,128)(2,1)}, bf16[512,512]{1,0:T(8,128)(2,1)S(1)}, u32[]{:S(2)}, u32[]{:S(2)}) collective-permute-start(bf16[512,512]{1,0:T(8,128)(2,1)} %collective-permute-done.8), channel_id=1, source_target_pairs={{0,4},{4,0},{8,12},{12,8},{16,20},{20,16},{24,28},{28,24},{1,5},{5... | collective-permute-start | bytes 1572872 | tf_op jit(solution)/shard_map/ppermute | solution.py:23
  232.0 57.9 %collective-permute-start.18 = (bf16[1536,1024]{1,0:T(8,128)(2,1)S(1)}, bf16[1536,1024]{1,0:T(8,128)(2,1)S(1)}, u32[]{:S(2)}, u32[]{:S(2)}) collective-permute-start(bf16[1536,1024]{1,0:T(8,128)(2,1)S(1)} %constant_dynamic-update-slice_fusion.24), channel_id=1, source_target_pairs={{0,1},{1,0},{2,3},{3,2},{4,5},{5,4},{6,7},{7,6},{8,9},{9,8},{10,11... | collective-permute-start | bytes 9437192 | tf_op jit(solution)/shard_map/ppermute | solution.py:30
  233.6 31.1 %collective-permute-start.30 = (bf16[512,512]{1,0:T(8,128)(2,1)S(1)}, bf16[512,512]{1,0:T(8,128)(2,1)S(1)}, u32[]{:S(2)}, u32[]{:S(2)}) collective-permute-start(bf16[512,512]{1,0:T(8,128)(2,1)S(1)} %collective-permute-done.26), channel_id=1, source_target_pairs={{0,4},{4,0},{8,12},{12,8},{16,20},{20,16},{24,28},{28,24},{1,5},{5... | collective-permute-start | bytes 1572872 | tf_op jit(solution)/shard_map/ppermute | solution.py:23
  242.2 30.7 %collective-permute-start.31 = (bf16[512,512]{1,0:T(8,128)(2,1)S(1)}, bf16[512,512]{1,0:T(8,128)(2,1)S(1)}, u32[]{:S(2)}, u32[]{:S(2)}) collective-permute-start(bf16[512,512]{1,0:T(8,128)(2,1)S(1)} %collective-permute-done.27), channel_id=1, source_target_pairs={{0,4},{4,0},{8,12},{12,8},{16,20},{20,16},{24,28},{28,24},{1,5},{5... | collective-permute-start | bytes 1572872 | tf_op jit(solution)/shard_map/ppermute | solution.py:23
  253.4 25.1 %collective-permute-start.32 = (bf16[512,512]{1,0:T(8,128)(2,1)S(1)}, bf16[512,512]{1,0:T(8,128)(2,1)S(1)}, u32[]{:S(2)}, u32[]{:S(2)}) collective-permute-start(bf16[512,512]{1,0:T(8,128)(2,1)S(1)} %collective-permute-done.28), channel_id=1, source_target_pairs={{0,4},{4,0},{8,12},{12,8},{16,20},{20,16},{24,28},{28,24},{1,5},{5... | collective-permute-start | bytes 1572872 | tf_op jit(solution)/shard_map/ppermute | solution.py:23
  335.8 36.5 %collective-permute-start.37 = (bf16[384,1024]{1,0:T(8,128)(2,1)S(1)}, bf16[384,1024]{1,0:T(8,128)(2,1)S(1)}, u32[]{:S(2)}, u32[]{:S(2)}) collective-permute-start(bf16[384,1024]{1,0:T(8,128)(2,1)S(1)} %slice.122), channel_id=1, source_target_pairs={{0,2},{2,0},{1,3},{3,1},{4,6},{6,4},{5,7},{7,5},{8,10},{10,8},{9,1... | collective-permute-start | bytes 2359304 | tf_op jit(solution)/shard_map/ppermute | solution.py:30
  336.9 50.5 %collective-permute-start.40 = (bf16[384,1024]{1,0:T(8,128)(2,1)S(1)}, bf16[384,1024]{1,0:T(8,128)(2,1)S(1)}, u32[]{:S(2)}, u32[]{:S(2)}) collective-permute-start(bf16[384,1024]{1,0:T(8,128)(2,1)S(1)} %slice.125), channel_id=1, source_target_pairs={{0,2},{2,0},{1,3},{3,1},{4,6},{6,4},{5,7},{7,5},{8,10},{10,8},{9,1... | collective-permute-start | bytes 2359304 | tf_op jit(solution)/shard_map/ppermute | solution.py:30
  339.5 73.2 %collective-permute-start.43 = (bf16[384,1024]{1,0:T(8,128)(2,1)S(1)}, bf16[384,1024]{1,0:T(8,128)(2,1)}, u32[]{:S(2)}, u32[]{:S(2)}) collective-permute-start(bf16[384,1024]{1,0:T(8,128)(2,1)S(1)} %slice.128), channel_id=1, source_target_pairs={{0,2},{2,0},{1,3},{3,1},{4,6},{6,4},{5,7},{7,5},{8,10},{10,8},{9,1... | collective-permute-start | bytes 2359304 | tf_op jit(solution)/shard_map/ppermute | solution.py:30
  354.1 58.6 %collective-permute-start.35 = (bf16[384,1024]{1,0:T(8,128)(2,1)S(1)}, bf16[384,1024]{1,0:T(8,128)(2,1)}, u32[]{:S(2)}, u32[]{:S(2)}) collective-permute-start(bf16[384,1024]{1,0:T(8,128)(2,1)S(1)} %add_convert_fusion.7), channel_id=1, source_target_pairs={{0,24},{4,28},{8,0},{12,4},{16,8},{20,12},{24,16},{28,20},{1,25},{... | collective-permute-start | bytes 2359304 | tf_op jit(solution)/shard_map/ppermute | solution.py:23
  372.6 65.2 %collective-permute-start.38 = (bf16[384,1024]{1,0:T(8,128)(2,1)S(1)}, bf16[384,1024]{1,0:T(8,128)(2,1)}, u32[]{:S(2)}, u32[]{:S(2)}) collective-permute-start(bf16[384,1024]{1,0:T(8,128)(2,1)S(1)} %add_convert_fusion.6), channel_id=1, source_target_pairs={{0,16},{4,20},{8,24},{12,28},{16,0},{20,4},{24,8},{28,12},{1,17},{... | collective-permute-start | bytes 2359304 | tf_op jit(solution)/shard_map/ppermute | solution.py:23
  388.7 49.1 %collective-permute-start.41 = (bf16[384,1024]{1,0:T(8,128)(2,1)}, bf16[384,1024]{1,0:T(8,128)(2,1)}, u32[]{:S(2)}, u32[]{:S(2)}) collective-permute-start(bf16[384,1024]{1,0:T(8,128)(2,1)} %add_convert_fusion.5), channel_id=1, source_target_pairs={{0,8},{4,12},{8,16},{12,20},{16,24},{20,28},{24,0},{28,4},{1,9},{5... | collective-permute-start | bytes 2359304 | tf_op jit(solution)/shard_map/ppermute | solution.py:23
  (31 other events, 1027.2 us)
